TPU v7x, 512 devices: a whole 4x4x16 slice. The times are simulated.
512 devices in a mesh: row: 8 (over y, x_hi), col: 16 (over z), layer: 4 (over x_lo, core).
Axes of the slice: x: 4 (x_hi: 2, x_lo: 2; x = x_hi * 2 + x_lo), y: 4, z: 16, core: 2. Of those that a mesh axis runs over, the one named last changes fastest.
Arguments:
- density: bfloat16 [2048, 16384], P('row', ('layer', 'col')), may hold values from -6 to 6
- margin: bfloat16 [16384, 16384], P(('layer', 'row'), 'col'), may hold values from -0.09375 to 0.09375
- block_pattern: int32 [128, 128], replicated, may hold values from 0 to 1, as said below
- atom_functions: int32 [512], replicated, may hold values from 1 to 9, 2048 in all
- atom_kind: int32 [512], P(('row', 'col', 'layer')), may hold values from 0 to 4
- atom_offset: float32 [3, 512], P(None, ('row', 'col', 'layer')), may hold values from 0 to 128, as said below
- exponents: float32 [5], replicated, may hold values from 0.02 to 1
Outputs:
- density_product: bfloat16 [2048, 16384], P('row', ('col', 'layer'))
- electron_density: float32 [256, 512, 512], P('row', 'col', 'layer')
Inputs may be any that keep to these rules, and one draw needn't show every extreme that they name: `block_pattern`: symmetric, with ones on its diagonal; block_pattern[i, j] = 0 whenever |i - j| > 32 (no block couples to one more than 32 blocks away). `atom_functions`: all atoms' functions together are the 2048 rows of the window. `atom_offset`: row k of an atom lies in [0, the tile's cells along dimension k), that is 32, 32 or 128.
All inputs are finite; a program needn't handle non-finite values.
Results may differ from a plain program's by a relative error of at most 0.001.
Values may be sent and summed in bfloat16 or wider, within the bound.
A program may use at most 64 MiB of HBM per device.

v0:
```python
import jax
import jax.numpy as jnp
from jax import lax
from jax.sharding import PartitionSpec as P

BLK = 128
TX = 32
TY = 32
TZ = 128
HALO = 16


def passed_along(block, axis, distance):
    devices = range(lax.axis_size(axis))
    route = [((i - distance) % len(devices), i) for i in devices]
    return lax.ppermute(block, axis, route)


def with_halo(block, sides, width):
    for axis, dim in sides:
        count = lax.axis_size(axis)
        forward = [(i, i + 1) for i in range(count - 1)]
        forward.append((count - 1, 0))
        backward = [(target, source) for source, target in forward]
        low = lax.ppermute(
            lax.slice_in_dim(block, block.shape[dim] - width, None, axis=dim), axis, forward
        )
        high = lax.ppermute(lax.slice_in_dim(block, 0, width, axis=dim), axis, backward)
        block = jnp.concatenate([low, block, high], axis=dim)
    return block


def apply_pattern(matrix, pattern_part):
    row_blocks = matrix.shape[0] // BLK
    col_blocks = matrix.shape[1] // BLK
    shaped = matrix.reshape(row_blocks, BLK, col_blocks, BLK)
    gate_mask = pattern_part.astype(jnp.bfloat16)
    return (shaped * gate_mask[:, None, :, None]).reshape(matrix.shape)


def local_profile(offset, exponent_of, extent):
    local_cells = jnp.arange(-HALO, extent + HALO, dtype=jnp.int32).astype(jnp.float32)
    distance = local_cells[None, :] - offset[:, None]
    return jnp.where(
        jnp.abs(distance) <= HALO, jnp.exp(-exponent_of[:, None] * distance * distance), 0.0
    )


def fold_rims(values_in, axis_dim, extent):
    middle = lax.slice_in_dim(values_in, 2 * HALO, 2 * HALO + extent, axis=axis_dim)
    lower_rim = lax.slice_in_dim(values_in, 0, HALO, axis=axis_dim)
    upper_rim = lax.slice_in_dim(values_in, extent + 3 * HALO, extent + 4 * HALO, axis=axis_dim)
    lower_edge = lax.slice_in_dim(middle, 0, HALO, axis=axis_dim) + lower_rim
    upper_edge = lax.slice_in_dim(middle, extent - HALO, extent, axis=axis_dim) + upper_rim
    inner_part = lax.slice_in_dim(middle, HALO, extent - HALO, axis=axis_dim)
    return jnp.concatenate([lower_edge, inner_part, upper_edge], axis=axis_dim)


def kind_exponent(kinds_of, exponents):
    kind_match = kinds_of[:, None] == jnp.arange(exponents.shape[0], dtype=jnp.int32)[None, :]
    return jnp.sum(jnp.where(kind_match, exponents[None, :], 0.0), axis=1)


def shards(density, margin, block_pattern, atom_functions, atom_kind, atom_offset, exponents):
    rows_here, piece_width = density.shape
    share_rows, share_cols = margin.shape
    n_row = lax.axis_size("row")
    n_col = lax.axis_size("col")
    n_layer = lax.axis_size("layer")
    row_index = lax.axis_index("row")
    col_index = lax.axis_index("col")
    layer_index = lax.axis_index("layer")
    density_mask = lax.dynamic_slice(
        block_pattern,
        (row_index * (rows_here // BLK), (layer_index * n_col + col_index) * piece_width // BLK),
        (rows_here // BLK, piece_width // BLK),
    )
    masked = apply_pattern(density, density_mask)
    margin_mask = lax.dynamic_slice(
        block_pattern,
        ((layer_index * n_row + row_index) * share_rows // BLK, col_index * share_cols // BLK),
        (share_rows // BLK, share_cols // BLK),
    )
    margin_masked = apply_pattern(margin, margin_mask)
    columns_panel = lax.all_gather(margin_masked, "row", axis=0, tiled=True)

    def add_piece(running, piece_rows, first_row):
        rows_of = lax.dynamic_slice_in_dim(columns_panel, first_row, piece_rows.shape[1], 0)
        return running + jnp.dot(piece_rows, rows_of, preferred_element_type=jnp.float32)

    product_zero = jnp.zeros((rows_here, share_cols), jnp.float32)

    def advance_one(turn_index, state_tuple):
        moving, running = state_tuple
        moving = passed_along(moving, "col", 1)
        return (
            moving,
            add_piece(running, moving, (col_index - turn_index - 1) % n_col * piece_width),
        )

    start_sum = add_piece(product_zero, masked, col_index * piece_width)
    product_acc = lax.fori_loop(0, n_col - 1, advance_one, (masked, start_sum))[1]
    product = lax.psum_scatter(product_acc, "layer", scatter_dimension=1, tiled=True)
    strip_width = product.shape[1]
    rows_global = row_index * rows_here + jnp.arange(rows_here, dtype=jnp.int32)
    cols_global = (col_index * n_layer + layer_index) * strip_width + jnp.arange(
        strip_width, dtype=jnp.int32
    )
    on_diagonal = rows_global[:, None] == cols_global[None, :]
    diagonal_part = jnp.sum(jnp.where(on_diagonal, product, 0.0), axis=0)
    run_ends = jnp.cumsum(atom_functions, dtype=jnp.int32)
    run_starts = run_ends - atom_functions
    member = (cols_global[:, None] >= run_starts[None, :]) & (
        cols_global[:, None] < run_ends[None, :]
    )
    partial_pop = jnp.dot(
        diagonal_part, member.astype(jnp.float32), precision=lax.Precision.HIGHEST
    )
    all_pop = lax.psum(partial_pop, ("row", "col", "layer"))
    slot_count = atom_kind.shape[0]
    tile_index = (row_index * n_col + col_index) * n_layer + layer_index
    own_pop = lax.dynamic_slice_in_dim(all_pop, tile_index * slot_count, slot_count, 0)
    exponent_of = kind_exponent(atom_kind, exponents)
    weight_x = own_pop[:, None] * local_profile(atom_offset[0], exponent_of, TX)
    along_y = local_profile(atom_offset[1], exponent_of, TY)
    along_z = local_profile(atom_offset[2], exponent_of, TZ)
    paired = weight_x[:, :, None] * along_y[:, None, :]
    extended = jnp.einsum("axy,az->xyz", paired, along_z, precision=lax.Precision.HIGHEST)
    summed = with_halo(extended, (("row", 0), ("col", 1), ("layer", 2)), HALO)
    electron_density = fold_rims(fold_rims(fold_rims(summed, 0, TX), 1, TY), 2, TZ)
    return (product.astype(jnp.bfloat16), electron_density)


def solution(mesh):
    placed = (
        P("row", ("layer", "col")),
        P(("layer", "row"), "col"),
        P(),
        P(),
        P(("row", "col", "layer")),
        P(None, ("row", "col", "layer")),
        P(),
    )
    return jax.shard_map(
        shards,
        mesh=mesh,
        in_specs=placed,
        out_specs=(P("row", ("col", "layer")), P("row", "col", "layer")),
        check_vma=False,
    )
```

profile of v0, /device:TPU:1, one launch (start us, length us, event | category | flops | bytes accessed | tf_op | source)
XLA Modules:
  0.0 577.8 jit_solution(15590409641228112352)
XLA Ops:
  10.6 127.0 %all-gather.2.cloned.1.call-done = bf16[4096,1024]{1,0:T(8,128)(2,1)} async-done(((bf16[512,1024]{1,0:T(8,128)(2,1)}), bf16[4096,1024]{1,0:T(8,128)(2,1)}) %all-gather.2.cloned.1.call-update) | async-done | bytes 8388624 | tf_op jit(solution)/shard_map/all_gather | solution.py:85
  139.1 129.6 %while.17 = (s32[]{:T(128)}, bf16[256,256]{1,0:T(8,128)(2,1)S(1)}, f32[256,1024]{0,1:T(8,128)S(1)}, s32[]{:T(128)}, bf16[4096,1024]{1,0:T(8,128)(2,1)}, /*index=...) while((s32[]{:T(128)}, bf16[256,256]{1,0:T(8,128)(2,1)S(1)}, ...), condition=%wide.region_1.2_spmd, body=%wide.region_0.1_spmd.sunk | while | flops 134479888 | bytes 3539284 | solution.py:102
  150.5 5.0 collective-permute-done
  158.9 5.0 collective-permute-done
  167.3 5.0 collective-permute-done
  175.7 5.0 collective-permute-done
  184.1 5.0 collective-permute-done
  192.4 5.3 collective-permute-done
  201.2 6.6 %collective-permute-done = bf16[256,256]{1,0:T(8,128)(2,1)S(1)} collective-permute-done((bf16[256,256]{1,0:T(8,128)(2,1)S(1)}, bf16[256,256]{1,0:T(8,128)(2,1)S(1)}, u32[]{:S(2)}, u32[]{:S(2)}) %collective-permute-start) | collective-permute-done | bytes 131104 | tf_op jit(solution)/shard_map/while/body/eval_jaxpr/ppermute | solution.py:16
  211.2 5.7 collective-permute-done
  220.3 5.0 collective-permute-done
  228.7 5.0 collective-permute-done
  237.1 5.0 collective-permute-done
  245.5 5.0 collective-permute-done
  253.8 5.0 collective-permute-done
  274.5 38.1 %reduce-scatter.2.cloned.1.call-done = f32[256,256]{1,0:T(8,128)} async-done(((f32[256,1024]{1,0:T(8,128)}), f32[256,256]{1,0:T(8,128)}) %reduce-scatter.2.cloned.1.call-update) | async-done | bytes 262160 | tf_op jit(solution)/shard_map/reduce_scatter | solution.py:103
  314.7 105.2 %psum.7 = f32[512]{0:T(512)S(1)} all-reduce(f32[512]{0:T(512)S(1)} %bitcast.36), channel_id=1, replica_groups=mesh['row'=8,'col'=16,'layer'=4] {'row','col','layer'}, use_global_device_ids=true, to_apply=%region_6.7 | all-reduce | flops 512 | bytes 4096 | tf_op jit(solution)/shard_map/psum | solution.py:119
  425.6 5.8 %collective-permute-start.2 = (f32[16,64,160]{2,1,0:T(8,128)S(1)}, f32[16,64,160]{2,1,0:T(8,128)S(1)}, u32[]{:S(2)}, u32[]{:S(2)}) collective-permute-start(f32[16,64,160]{2,1,0:T(8,128)S(1)} %get-tuple-element.176), channel_id=1, source_target_pairs={{64,0},{128,64},{192,128},{256,192},{320,256},{384,320},{448,384},... | collective-permute-start | bytes 1966088 | tf_op jit(solution)/shard_map/ppermute | solution.py:28
  431.4 20.6 %collective-permute-done.1 = f32[16,64,160]{2,1,0:T(8,128)S(1)} collective-permute-done((f32[16,64,160]{2,1,0:T(8,128)S(1)}, f32[16,64,160]{2,1,0:T(8,128)S(1)}, u32[]{:S(2)}, u32[]{:S(2)}) %collective-permute-start.1) | collective-permute-done | bytes 655392 | tf_op jit(solution)/shard_map/ppermute | solution.py:25
  452.1 19.8 %collective-permute-done.2 = f32[16,64,160]{2,1,0:T(8,128)S(1)} collective-permute-done((f32[16,64,160]{2,1,0:T(8,128)S(1)}, f32[16,64,160]{2,1,0:T(8,128)S(1)}, u32[]{:S(2)}, u32[]{:S(2)}) %collective-permute-start.2) | collective-permute-done | bytes 655392 | tf_op jit(solution)/shard_map/ppermute | solution.py:28
  484.1 23.6 %collective-permute-done.4 = f32[96,16,160]{0,2,1:T(8,128)} collective-permute-done((f32[96,16,160]{0,2,1:T(8,128)}, f32[96,16,160]{0,2,1:T(8,128)}, u32[]{:S(2)}, u32[]{:S(2)}) %collective-permute-start.4) | collective-permute-done | bytes 983072 | tf_op jit(solution)/shard_map/ppermute | solution.py:28
  521.0 5.3 fusion.24
  547.7 6.4 %collective-permute-done.6 = f32[96,96,16]{1,2,0:T(8,128)} collective-permute-done((f32[96,96,16]{1,2,0:T(8,128)}, f32[96,96,16]{1,2,0:T(8,128)}, u32[]{:S(2)}, u32[]{:S(2)}) %collective-permute-start.6) | collective-permute-done | bytes 589856 | tf_op jit(solution)/shard_map/ppermute | solution.py:28
  558.0 5.8 %maximum_add_fusion = f32[16,96,192]{2,1,0:T(8,128)S(1)} fusion(f32[96,96,16]{2,1,0:T(8,128)} %copy.29, f32[96,96,16]{2,1,0:T(8,128)} %copy.28, f32[96,16,160]{2,1,0:T(8,128)S(1)} %copy.25, f32[96,16,160]{2,1,0:T(8,128)} %copy.24, f32[16,64,160]{2,1,0:T(8,128)} %copy-done.4, f32[64,64,160]{2,1,0:T(8,128)} %copy-done, ...), kind=kLoop, calls=%fused_computation.21 | loop fusion | flops 3833856 | bytes 8257536 | tf_op jit(solution)/shard_map/add | solution.py:53
  (125 shorter events, 136.1 us)
Async XLA Ops:
  7.2 130.5 %all-gather.2.cloned.1.call-start = ((), (), s32[]{:S(2)}) async-start(), calls=%async_computation.1 | async-start | bytes 9437184 | tf_op jit(solution)/shard_map/all_gather | solution.py:85
  9.6 303.0 %reduce-scatter.2.cloned.1.call-start = ((), (), s32[]{:S(2)}) async-start(), calls=%async_computation.2 | async-start | bytes 1310720 | tf_op jit(solution)/shard_map/reduce_scatter | solution.py:103
  139.1 8.0 %collective-permute-start = (bf16[256,256]{1,0:T(8,128)(2,1)S(1)}, bf16[256,256]{1,0:T(8,128)(2,1)S(1)}, u32[]{:S(2)}, u32[]{:S(2)}) collective-permute-start(bf16[256,256]{1,0:T(8,128)(2,1)S(1)} %get-tuple-element.232), channel_id=1, source_target_pairs={{60,0},{0,4},{4,8},{8,12},{12,16},{16,20},{20,24},{24,28},{28,32},... | collective-permute-start | bytes 393224 | tf_op jit(solution)/shard_map/while/body/eval_jaxpr/ppermute | solution.py:16
  148.6 6.9 %collective-permute-start = (bf16[256,256]{1,0:T(8,128)(2,1)S(1)}, bf16[256,256]{1,0:T(8,128)(2,1)S(1)}, u32[]{:S(2)}, u32[]{:S(2)}) collective-permute-start(bf16[256,256]{1,0:T(8,128)(2,1)S(1)} %get-tuple-element.232), channel_id=1, source_target_pairs={{60,0},{0,4},{4,8},{8,12},{12,16},{16,20},{20,24},{24,28},{28,32},... | collective-permute-start | bytes 393224 | tf_op jit(solution)/shard_map/while/body/eval_jaxpr/ppermute | solution.py:16
  157.0 6.9 %collective-permute-start = (bf16[256,256]{1,0:T(8,128)(2,1)S(1)}, bf16[256,256]{1,0:T(8,128)(2,1)S(1)}, u32[]{:S(2)}, u32[]{:S(2)}) collective-permute-start(bf16[256,256]{1,0:T(8,128)(2,1)S(1)} %get-tuple-element.232), channel_id=1, source_target_pairs={{60,0},{0,4},{4,8},{8,12},{12,16},{16,20},{20,24},{24,28},{28,32},... | collective-permute-start | bytes 393224 | tf_op jit(solution)/shard_map/while/body/eval_jaxpr/ppermute | solution.py:16
  165.3 6.9 %collective-permute-start = (bf16[256,256]{1,0:T(8,128)(2,1)S(1)}, bf16[256,256]{1,0:T(8,128)(2,1)S(1)}, u32[]{:S(2)}, u32[]{:S(2)}) collective-permute-start(bf16[256,256]{1,0:T(8,128)(2,1)S(1)} %get-tuple-element.232), channel_id=1, source_target_pairs={{60,0},{0,4},{4,8},{8,12},{12,16},{16,20},{20,24},{24,28},{28,32},... | collective-permute-start | bytes 393224 | tf_op jit(solution)/shard_map/while/body/eval_jaxpr/ppermute | solution.py:16
  173.7 6.9 %collective-permute-start = (bf16[256,256]{1,0:T(8,128)(2,1)S(1)}, bf16[256,256]{1,0:T(8,128)(2,1)S(1)}, u32[]{:S(2)}, u32[]{:S(2)}) collective-permute-start(bf16[256,256]{1,0:T(8,128)(2,1)S(1)} %get-tuple-element.232), channel_id=1, source_target_pairs={{60,0},{0,4},{4,8},{8,12},{12,16},{16,20},{20,24},{24,28},{28,32},... | collective-permute-start | bytes 393224 | tf_op jit(solution)/shard_map/while/body/eval_jaxpr/ppermute | solution.py:16
  182.1 6.9 %collective-permute-start = (bf16[256,256]{1,0:T(8,128)(2,1)S(1)}, bf16[256,256]{1,0:T(8,128)(2,1)S(1)}, u32[]{:S(2)}, u32[]{:S(2)}) collective-permute-start(bf16[256,256]{1,0:T(8,128)(2,1)S(1)} %get-tuple-element.232), channel_id=1, source_target_pairs={{60,0},{0,4},{4,8},{8,12},{12,16},{16,20},{20,24},{24,28},{28,32},... | collective-permute-start | bytes 393224 | tf_op jit(solution)/shard_map/while/body/eval_jaxpr/ppermute | solution.py:16
  190.5 7.3 %collective-permute-start = (bf16[256,256]{1,0:T(8,128)(2,1)S(1)}, bf16[256,256]{1,0:T(8,128)(2,1)S(1)}, u32[]{:S(2)}, u32[]{:S(2)}) collective-permute-start(bf16[256,256]{1,0:T(8,128)(2,1)S(1)} %get-tuple-element.232), channel_id=1, source_target_pairs={{60,0},{0,4},{4,8},{8,12},{12,16},{16,20},{20,24},{24,28},{28,32},... | collective-permute-start | bytes 393224 | tf_op jit(solution)/shard_map/while/body/eval_jaxpr/ppermute | solution.py:16
  199.2 8.5 %collective-permute-start = (bf16[256,256]{1,0:T(8,128)(2,1)S(1)}, bf16[256,256]{1,0:T(8,128)(2,1)S(1)}, u32[]{:S(2)}, u32[]{:S(2)}) collective-permute-start(bf16[256,256]{1,0:T(8,128)(2,1)S(1)} %get-tuple-element.232), channel_id=1, source_target_pairs={{60,0},{0,4},{4,8},{8,12},{12,16},{16,20},{20,24},{24,28},{28,32},... | collective-permute-start | bytes 393224 | tf_op jit(solution)/shard_map/while/body/eval_jaxpr/ppermute | solution.py:16
  209.2 7.7 %collective-permute-start = (bf16[256,256]{1,0:T(8,128)(2,1)S(1)}, bf16[256,256]{1,0:T(8,128)(2,1)S(1)}, u32[]{:S(2)}, u32[]{:S(2)}) collective-permute-start(bf16[256,256]{1,0:T(8,128)(2,1)S(1)} %get-tuple-element.232), channel_id=1, source_target_pairs={{60,0},{0,4},{4,8},{8,12},{12,16},{16,20},{20,24},{24,28},{28,32},... | collective-permute-start | bytes 393224 | tf_op jit(solution)/shard_map/while/body/eval_jaxpr/ppermute | solution.py:16
  218.3 6.9 %collective-permute-start = (bf16[256,256]{1,0:T(8,128)(2,1)S(1)}, bf16[256,256]{1,0:T(8,128)(2,1)S(1)}, u32[]{:S(2)}, u32[]{:S(2)}) collective-permute-start(bf16[256,256]{1,0:T(8,128)(2,1)S(1)} %get-tuple-element.232), channel_id=1, source_target_pairs={{60,0},{0,4},{4,8},{8,12},{12,16},{16,20},{20,24},{24,28},{28,32},... | collective-permute-start | bytes 393224 | tf_op jit(solution)/shard_map/while/body/eval_jaxpr/ppermute | solution.py:16
  226.7 6.9 %collective-permute-start = (bf16[256,256]{1,0:T(8,128)(2,1)S(1)}, bf16[256,256]{1,0:T(8,128)(2,1)S(1)}, u32[]{:S(2)}, u32[]{:S(2)}) collective-permute-start(bf16[256,256]{1,0:T(8,128)(2,1)S(1)} %get-tuple-element.232), channel_id=1, source_target_pairs={{60,0},{0,4},{4,8},{8,12},{12,16},{16,20},{20,24},{24,28},{28,32},... | collective-permute-start | bytes 393224 | tf_op jit(solution)/shard_map/while/body/eval_jaxpr/ppermute | solution.py:16
  235.1 6.9 %collective-permute-start = (bf16[256,256]{1,0:T(8,128)(2,1)S(1)}, bf16[256,256]{1,0:T(8,128)(2,1)S(1)}, u32[]{:S(2)}, u32[]{:S(2)}) collective-permute-start(bf16[256,256]{1,0:T(8,128)(2,1)S(1)} %get-tuple-element.232), channel_id=1, source_target_pairs={{60,0},{0,4},{4,8},{8,12},{12,16},{16,20},{20,24},{24,28},{28,32},... | collective-permute-start | bytes 393224 | tf_op jit(solution)/shard_map/while/body/eval_jaxpr/ppermute | solution.py:16
  243.5 6.9 %collective-permute-start = (bf16[256,256]{1,0:T(8,128)(2,1)S(1)}, bf16[256,256]{1,0:T(8,128)(2,1)S(1)}, u32[]{:S(2)}, u32[]{:S(2)}) collective-permute-start(bf16[256,256]{1,0:T(8,128)(2,1)S(1)} %get-tuple-element.232), channel_id=1, source_target_pairs={{60,0},{0,4},{4,8},{8,12},{12,16},{16,20},{20,24},{24,28},{28,32},... | collective-permute-start | bytes 393224 | tf_op jit(solution)/shard_map/while/body/eval_jaxpr/ppermute | solution.py:16
  251.9 6.9 %collective-permute-start = (bf16[256,256]{1,0:T(8,128)(2,1)S(1)}, bf16[256,256]{1,0:T(8,128)(2,1)S(1)}, u32[]{:S(2)}, u32[]{:S(2)}) collective-permute-start(bf16[256,256]{1,0:T(8,128)(2,1)S(1)} %get-tuple-element.232), channel_id=1, source_target_pairs={{60,0},{0,4},{4,8},{8,12},{12,16},{16,20},{20,24},{24,28},{28,32},... | collective-permute-start | bytes 393224 | tf_op jit(solution)/shard_map/while/body/eval_jaxpr/ppermute | solution.py:16
  260.3 6.9 %collective-permute-start = (bf16[256,256]{1,0:T(8,128)(2,1)S(1)}, bf16[256,256]{1,0:T(8,128)(2,1)S(1)}, u32[]{:S(2)}, u32[]{:S(2)}) collective-permute-start(bf16[256,256]{1,0:T(8,128)(2,1)S(1)} %get-tuple-element.232), channel_id=1, source_target_pairs={{60,0},{0,4},{4,8},{8,12},{12,16},{16,20},{20,24},{24,28},{28,32},... | collective-permute-start | bytes 393224 | tf_op jit(solution)/shard_map/while/body/eval_jaxpr/ppermute | solution.py:16
  422.4 49.5 %copy-start = (f32[64,64,160]{2,1,0:T(8,128)}, f32[64,64,160]{2,1,0:T(8,128)S(1)}, u32[]{:S(2)}) copy-start(f32[64,64,160]{2,1,0:T(8,128)S(1)} %broadcast_multiply_fusion) | copy-start | bytes 7864324
  422.5 29.6 %collective-permute-start.1 = (f32[16,64,160]{2,1,0:T(8,128)S(1)}, f32[16,64,160]{2,1,0:T(8,128)S(1)}, u32[]{:S(2)}, u32[]{:S(2)}) collective-permute-start(f32[16,64,160]{2,1,0:T(8,128)S(1)} %get-tuple-element.175), channel_id=1, source_target_pairs={{0,64},{64,128},{128,192},{192,256},{256,320},{320,384},{384,448},... | collective-permute-start | bytes 1966088 | tf_op jit(solution)/shard_map/ppermute | solution.py:25
  425.6 46.3 %collective-permute-start.2 = (f32[16,64,160]{2,1,0:T(8,128)S(1)}, f32[16,64,160]{2,1,0:T(8,128)S(1)}, u32[]{:S(2)}, u32[]{:S(2)}) collective-permute-start(f32[16,64,160]{2,1,0:T(8,128)S(1)} %get-tuple-element.176), channel_id=1, source_target_pairs={{64,0},{128,64},{192,128},{256,192},{320,256},{384,320},{448,384},... | collective-permute-start | bytes 1966088 | tf_op jit(solution)/shard_map/ppermute | solution.py:28
  476.7 31.0 %collective-permute-start.4 = (f32[96,16,160]{0,2,1:T(8,128)}, f32[96,16,160]{0,2,1:T(8,128)}, u32[]{:S(2)}, u32[]{:S(2)}) collective-permute-start(f32[96,16,160]{0,2,1:T(8,128)} %copy.23), channel_id=1, source_target_pairs={{4,0},{8,4},{12,8},{16,12},{20,16},{24,20},{28,24},{32,28},{36,32}... | collective-permute-start | bytes 2949128 | tf_op jit(solution)/shard_map/ppermute | solution.py:28
  481.8 31.9 %collective-permute-start.3 = (f32[96,16,160]{0,2,1:T(8,128)}, f32[96,16,160]{0,2,1:T(8,128)}, u32[]{:S(2)}, u32[]{:S(2)}) collective-permute-start(f32[96,16,160]{0,2,1:T(8,128)} %copy.22), channel_id=1, source_target_pairs={{0,4},{4,8},{8,12},{12,16},{16,20},{20,24},{24,28},{28,32},{32,36}... | collective-permute-start | bytes 2949128 | tf_op jit(solution)/shard_map/ppermute | solution.py:25
  530.1 13.8 %collective-permute-start.5 = (f32[96,96,16]{1,2,0:T(8,128)}, f32[96,96,16]{1,2,0:T(8,128)}, u32[]{:S(2)}, u32[]{:S(2)}) collective-permute-start(f32[96,96,16]{1,2,0:T(8,128)} %copy.26), channel_id=1, source_target_pairs={{0,1},{1,2},{2,3},{3,0},{4,5},{5,6},{6,7},{7,4},{8,9},{9,10},{10,1... | collective-permute-start | bytes 1769480 | tf_op jit(solution)/shard_map/ppermute | solution.py:25
  538.1 16.0 %collective-permute-start.6 = (f32[96,96,16]{1,2,0:T(8,128)}, f32[96,96,16]{1,2,0:T(8,128)}, u32[]{:S(2)}, u32[]{:S(2)}) collective-permute-start(f32[96,96,16]{1,2,0:T(8,128)} %copy.27), channel_id=1, source_target_pairs={{1,0},{2,1},{3,2},{0,3},{5,4},{6,5},{7,6},{4,7},{9,8},{10,9},{11,1... | collective-permute-start | bytes 1769480 | tf_op jit(solution)/shard_map/ppermute | solution.py:28
  (12 other events, 55.3 us)
Sparse Core Ops, SparseCore 0:
  11.2 126.4 all-gather.1
  270.1 42.3 reduce-scatter.1
where the time goes:
time: 580 us; the launch traced here: 578 us
  waiting for transfers between devices  319 us (55%)
  blocking collectives  105 us (18%)
  starting transfers between devices  51 us (9%)
  local copies, waits for them, and re-layouts  36.6 us (6%)
  other arithmetic  25.9 us (4%)
  matrix products  23.1 us (4%)
  between operations  15.7 us (3%)
    all_gather x1, waiting for transfers between devices, shards(): columns_panel = lax.all_gather(margin_masked, 'row', axis=0, tiled=True)  127 us
    psum x1, blocking collectives, shards(): all_pop = lax.psum(partial_pop, ('row', 'col', 'layer'))  105 us
    ppermute x15, waiting for transfers between devices, passed_along(): return lax.ppermute(block, axis, route)  77.1 us
    ppermute x3, waiting for transfers between devices, with_halo(): lax.ppermute(lax.slice_in_dim(block, 0, width, axis=dim), axis, backward)  49.8 us
    reduce_scatter x1, waiting for transfers between devices, shards(): lax.psum_scatter(product_acc, 'layer', scatter_dimension=1, tiled=True)  38.1 us
    ppermute x15, starting transfers between devices, passed_along(): return lax.ppermute(block, axis, route)  30.1 us
    ppermute x3, waiting for transfers between devices, with_halo(): lax.ppermute(lax.slice_in_dim(block, block.shape[dim] - width, None, axis...  27.3 us
    dot_general x16, matrix products, add_piece(): jnp.dot(piece_rows, rows_of, preferred_element_type=jnp.float32)  22.8 us
  transfers between devices with their start and end apart: 23, of which 23 were waited for; matrix products, arithmetic and copies ran while one was open for 3% of the time, Pallas kernels for 0%

commit v1 on v0

v1 whole, which is shorter than its diff:
```python
import jax
import jax.numpy as jnp
from jax import lax
from jax.experimental import pallas as pl
from jax.experimental.pallas import tpu as pltpu
from jax.sharding import PartitionSpec as P

BLK = 128
TX = 32
TY = 32
TZ = 128
HALO = 16

MESH = pl.DeviceIdType.MESH


def spread_kernel(part_ref, out_ref, mine, slots, send_a, recv_a, send_b, recv_b):
    row = lax.axis_index("row")
    col = lax.axis_index("col")
    layer = lax.axis_index("layer")
    n_row = slots.shape[0]
    n_layer = lax.axis_size("layer")
    others = lax.axis_size("col") * n_layer
    home_col = row // n_layer
    home_layer = row % n_layer
    home = (col == home_col) & (layer == home_layer)
    barrier = pltpu.get_barrier_semaphore()

    @pl.when(jnp.logical_not(home))
    def _():
        pl.semaphore_signal(
            barrier, inc=1, device_id=(row, home_col, home_layer), device_id_type=MESH
        )

    for step in range(1, n_row):
        mate = (row + step) % n_row
        pl.semaphore_signal(barrier, inc=1, device_id=(mate, col, layer), device_id_type=MESH)

    def copy_a(index):
        return pltpu.make_async_remote_copy(
            src_ref=part_ref,
            dst_ref=mine,
            send_sem=send_a.at[index],
            recv_sem=recv_a,
            device_id=(row, index // n_layer, index % n_layer),
            device_id_type=MESH,
        )

    def copies_b(source):
        return [
            pltpu.make_async_remote_copy(
                src_ref=source,
                dst_ref=slots.at[row],
                send_sem=send_b.at[step],
                recv_sem=recv_b.at[row],
                device_id=((row + step) % n_row, col, layer),
                device_id_type=MESH,
            )
            for step in range(1, n_row)
        ]

    @pl.when(home)
    def _():
        pl.semaphore_wait(barrier, others - 1 + n_row - 1)
        for copy in copies_b(part_ref):
            copy.start()
        own = col * n_layer + layer

        def send_one(step, carry):
            copy_a((own + step) % others).start()
            return carry

        def end_one(step, carry):
            copy_a((own + step) % others).wait_send()
            return carry

        lax.fori_loop(1, others, send_one, 0)
        lax.fori_loop(1, others, end_one, 0)
        for copy in copies_b(part_ref):
            copy.wait_send()

    @pl.when(jnp.logical_not(home))
    def _():
        pl.semaphore_wait(barrier, n_row - 1)
        copy_a(0).wait_recv()
        for copy in copies_b(mine):
            copy.start()
        for copy in copies_b(mine):
            copy.wait_send()

    for step in range(1, n_row):
        mate = (row + step) % n_row
        pltpu.make_async_remote_copy(
            src_ref=part_ref,
            dst_ref=slots.at[mate],
            send_sem=send_b.at[0],
            recv_sem=recv_b.at[mate],
            device_id=(mate, col, layer),
            device_id_type=MESH,
        ).wait_recv()

    @pl.when(home)
    def _():
        out_ref[...] = part_ref[...]

    @pl.when(jnp.logical_not(home))
    def _():
        out_ref[...] = mine[...]

    for step in range(1, n_row):
        out_ref[...] += slots[(row + step) % n_row]


def spread(part):
    n_row = lax.axis_size("row")
    others = lax.axis_size("col") * lax.axis_size("layer")
    return pl.pallas_call(
        spread_kernel,
        out_shape=jax.ShapeDtypeStruct(part.shape, part.dtype),
        in_specs=[pl.BlockSpec(memory_space=pltpu.VMEM)],
        out_specs=pl.BlockSpec(memory_space=pltpu.VMEM),
        scratch_shapes=[
            pltpu.VMEM(part.shape, part.dtype),
            pltpu.VMEM((n_row,) + part.shape, part.dtype),
            pltpu.SemaphoreType.DMA((others,)),
            pltpu.SemaphoreType.DMA,
            pltpu.SemaphoreType.DMA((n_row,)),
            pltpu.SemaphoreType.DMA((n_row,)),
        ],
        compiler_params=pltpu.CompilerParams(collective_id=0, has_side_effects=True),
    )(part)


def with_neighbours(block, axis):
    count = lax.axis_size(axis)
    upward = [(i, (i + 1) % count) for i in range(count)]
    downward = [(target, source) for source, target in upward]
    below = lax.ppermute(block, axis, upward)
    above = lax.ppermute(block, axis, downward)
    return jnp.concatenate([below, block, above], axis=0)


def near_profile(cells, tile_of, extent, offset, exponent_of):
    local = jnp.arange(cells, dtype=jnp.int32)[None, :] - tile_of[:, None] * extent
    distance = local.astype(jnp.float32) - offset[:, None]
    return jnp.where(
        jnp.abs(distance) <= HALO, jnp.exp(-exponent_of[:, None] * distance * distance), 0.0
    )


def collocate(near, weights):
    index = jnp.arange(27, dtype=jnp.int32)
    exponent_of = near[:, 0]
    along_x = near_profile(TX, index % 3 - 1, TX, near[:, 1], exponent_of)
    along_y = near_profile(TY, index // 3 % 3 - 1, TY, near[:, 2], exponent_of)
    along_z = near_profile(TZ, index // 9 - 1, TZ, near[:, 3], exponent_of)
    paired = (weights[:, None] * along_x)[:, :, None] * along_y[:, None, :]
    return jnp.einsum("axy,az->xyz", paired, along_z, precision=lax.Precision.HIGHEST)


def shards(density, margin, block_pattern, atom_functions, atom_kind, atom_offset, exponents):
    rows_here, piece_width = density.shape
    share_rows, share_cols = margin.shape
    n_row = lax.axis_size("row")
    n_col = lax.axis_size("col")
    n_layer = lax.axis_size("layer")
    row_index = lax.axis_index("row")
    col_index = lax.axis_index("col")
    layer_index = lax.axis_index("layer")
    exponent_here = kind_exponent(atom_kind, exponents)
    near = jnp.concatenate([exponent_here[:, None], atom_offset.T], axis=1)
    for axis in ("row", "col", "layer"):
        near = with_neighbours(near, axis)
    density_mask = lax.dynamic_slice(
        block_pattern,
        (row_index * (rows_here // BLK), (layer_index * n_col + col_index) * piece_width // BLK),
        (rows_here // BLK, piece_width // BLK),
    )
    masked = apply_pattern(density, density_mask)
    margin_mask = lax.dynamic_slice(
        block_pattern,
        ((layer_index * n_row + row_index) * share_rows // BLK, col_index * share_cols // BLK),
        (share_rows // BLK, share_cols // BLK),
    )
    margin_masked = apply_pattern(margin, margin_mask)
    paired_rows = margin_masked.reshape(share_rows // (2 * BLK), 2, BLK, share_cols)
    lend = [(0, 2), (1, 3)]
    lender = layer_index < 2
    margin_lent = lax.ppermute(paired_rows[:, 1], "layer", lend)
    density_lent = lax.ppermute(masked[:, BLK:], "layer", lend)
    margin_half = jnp.where(lender, paired_rows[:, 0], margin_lent).reshape(-1, share_cols)
    density_half = jnp.where(lender, masked[:, :BLK], density_lent)
    density_all = lax.all_gather(density_half, "col", axis=1, tiled=True)
    margin_all = lax.all_gather(margin_half, "row", axis=0, tiled=True)
    product_acc = jnp.dot(density_all, margin_all, preferred_element_type=jnp.float32)
    product = lax.psum_scatter(product_acc, "layer", scatter_dimension=1, tiled=True)
    strip_width = product.shape[1]
    rows_global = row_index * rows_here + jnp.arange(rows_here, dtype=jnp.int32)
    cols_global = (col_index * n_layer + layer_index) * strip_width + jnp.arange(
        strip_width, dtype=jnp.int32
    )
    on_diagonal = rows_global[:, None] == cols_global[None, :]
    diagonal_part = jnp.sum(jnp.where(on_diagonal, product, 0.0), axis=0)
    run_ends = jnp.cumsum(atom_functions, dtype=jnp.int32)
    run_starts = run_ends - atom_functions
    member = (cols_global[:, None] >= run_starts[None, :]) & (
        cols_global[:, None] < run_ends[None, :]
    )
    partial_pop = jnp.sum(jnp.where(member, diagonal_part[:, None], 0.0), axis=0)
    all_pop = spread(partial_pop.reshape(-1, 128)).reshape(-1)
    index = jnp.arange(27, dtype=jnp.int32)
    near_atom = (
        ((row_index + index % 3 - 1) % n_row) * n_col + (col_index + index // 3 % 3 - 1) % n_col
    ) * n_layer + (layer_index + index // 9 - 1) % n_layer
    atoms = jnp.arange(all_pop.shape[0], dtype=jnp.int32)
    weights = jnp.sum(jnp.where(near_atom[:, None] == atoms[None, :], all_pop[None, :], 0.0), axis=1)
    return (product.astype(jnp.bfloat16), collocate(near, weights))


def apply_pattern(matrix, pattern_part):
    row_blocks = matrix.shape[0] // BLK
    col_blocks = matrix.shape[1] // BLK
    shaped = matrix.reshape(row_blocks, BLK, col_blocks, BLK)
    gate_mask = pattern_part.astype(jnp.bfloat16)
    return (shaped * gate_mask[:, None, :, None]).reshape(matrix.shape)


def kind_exponent(kinds_of, exponents):
    kind_match = kinds_of[:, None] == jnp.arange(exponents.shape[0], dtype=jnp.int32)[None, :]
    return jnp.sum(jnp.where(kind_match, exponents[None, :], 0.0), axis=1)


def solution(mesh):
    placed = (
        P("row", ("layer", "col")),
        P(("layer", "row"), "col"),
        P(),
        P(),
        P(("row", "col", "layer")),
        P(None, ("row", "col", "layer")),
        P(),
    )
    return jax.shard_map(
        shards,
        mesh=mesh,
        in_specs=placed,
        out_specs=(P("row", ("col", "layer")), P("row", "col", "layer")),
        check_vma=False,
    )
```

time: 580 us -> 250 us (0.43)
  waiting for transfers between devices: 319 us -> 161 us
  blocking collectives: 105 us -> 0 us
  local copies, waits for them, and re-layouts: 36.6 us -> 1.14 us
  Pallas kernels: 0 us -> 24 us
  starting transfers between devices: 51 us -> 31.5 us
  matrix products: 23.1 us -> 6.16 us
  other arithmetic: 25.9 us -> 11.2 us
    ppermute x21 -> x8, waiting for transfers between devices: 154 us -> 10.8 us  [the longest x1 6.08 us: shards(): margin_lent = lax.ppermute(paired_rows[:, 1], 'layer', lend)]
    psum x1 -> x0, blocking collectives: 105 us -> none  [shards(): all_pop = lax.psum(partial_pop, ('row', 'col', 'layer'))]
    reduce_scatter x1, waiting for transfers between devices: 38.1 us -> 0.01 us  [shards(): lax.psum_scatter(product_acc, 'layer', scatter_dimension=1, tiled=True)]
    pallas_call x0 -> x1, Pallas kernels: none -> 24 us  [spread(): pl.pallas_call(spread_kernel, out_shape=jax.ShapeDtypeStruct(part.shape,...]
    all_gather x1 -> x2, waiting for transfers between devices: 127 us -> 150 us  [the longest x1 97 us: shards(): margin_all = lax.all_gather(margin_half, 'row', axis=0, tiled=True)]
    ppermute x21 -> x8, starting transfers between devices: 50.9 us -> 31.4 us  [the longest x3 13 us: with_neighbours(): above = lax.ppermute(block, axis, downward)]
    slice x8 -> x2, local copies, waits for them, and re-layouts: 19.1 us -> 0.08 us  [the longest x4 11.3 us: with_halo(): lax.slice_in_dim(block, block.shape[dim] - width, None, axis=dim)]
    dot_general x17 -> x2, matrix products: 23.1 us -> 6.16 us  [the longest x1 4.73 us: shards(): jnp.dot(density_all, margin_all, preferred_element_type=jnp.float32)]
  transfers between devices with their start and end apart: 23 -> 11, of which waited for: 23 -> 6; matrix products, arithmetic and copies ran while one was open for 3% -> 3% of each run, Pallas kernels for 0% -> 0%
where the time goes in v1:
time: 250 us; the launch traced here: 249 us
  waiting for transfers between devices  161 us (64%)
  starting transfers between devices  31.5 us (13%)
  Pallas kernels  24 us (10%)
  between operations  14.7 us (6%)
  other arithmetic  11.2 us (4%)
  matrix products  6.16 us (2%)
    all_gather x1, waiting for transfers between devices, shards(): margin_all = lax.all_gather(margin_half, 'row', axis=0, tiled=True)  97 us
    all_gather x1, waiting for transfers between devices, shards(): density_all = lax.all_gather(density_half, 'col', axis=1, tiled=True)  52.9 us
    pallas_call x1, Pallas kernels, spread(): pl.pallas_call(spread_kernel, out_shape=jax.ShapeDtypeStruct(part.shape,...  24 us
    ppermute x3, starting transfers between devices, with_neighbours(): above = lax.ppermute(block, axis, downward)  13 us
    ppermute x3, starting transfers between devices, with_neighbours(): below = lax.ppermute(block, axis, upward)  10.7 us
    ppermute x1, waiting for transfers between devices, shards(): margin_lent = lax.ppermute(paired_rows[:, 1], 'layer', lend)  6.08 us
  transfers between devices with their start and end apart: 11, of which 6 were waited for; matrix products, arithmetic and copies ran while one was open for 3% of the time, Pallas kernels for 0%

profile of v1, /device:TPU:1, one launch (start us, length us, event | category | flops | bytes accessed | tf_op | source)
XLA Modules:
  0.0 249.4 jit_solution(17250584048280831393)
XLA Ops:
  7.2 0.8 dynamic-slice_convert_fusion.1
  8.1 0.9 bitcast_multiply_fusion
  9.1 3.9 %collective-permute-start = (bf16[256,128]{1,0:T(8,128)(2,1)S(1)}, bf16[256,128]{1,0:T(8,128)(2,1)S(1)}, u32[]{:S(2)}, u32[]{:S(2)}) collective-permute-start(bf16[256,128]{1,0:T(8,128)(2,1)S(1)} %slice.45), channel_id=1, source_target_pairs={{0,2},{1,3},{4,6},{5,7},{8,10},{9,11},{12,14},{13,15},{16,18},{17,... | collective-permute-start | bytes 196616 | tf_op jit(solution)/shard_map/ppermute | solution.py:190
  13.0 1.3 collective-permute-done
  15.1 0.8 dynamic-slice_convert_fusion
  16.0 1.3 broadcast_multiply_fusion
  17.3 3.7 %collective-permute-start.1 = (bf16[2,128,1024]{2,1,0:T(8,128)(2,1)S(1)}, bf16[2,128,1024]{2,1,0:T(8,128)(2,1)S(1)}, u32[]{:S(2)}, u32[]{:S(2)}) collective-permute-start(bf16[2,128,1024]{2,1,0:T(8,128)(2,1)S(1)} %slice_bitcast_fusion), channel_id=1, source_target_pairs={{0,2},{1,3},{4,6},{5,7},{8,10},{9,11},{12,14},{13,15},{16,18},{17,... | collective-permute-start | bytes 1572872 | tf_op jit(solution)/shard_map/ppermute | solution.py:189
  21.0 6.1 %collective-permute-done.1 = bf16[2,128,1024]{2,1,0:T(8,128)(2,1)S(1)} collective-permute-done((bf16[2,128,1024]{2,1,0:T(8,128)(2,1)S(1)}, bf16[2,128,1024]{2,1,0:T(8,128)(2,1)S(1)}, u32[]{:S(2)}, u32[]{:S(2)}) %collective-permute-start.1) | collective-permute-done | bytes 524320 | tf_op jit(solution)/shard_map/ppermute | solution.py:189
  27.1 0.9 fusion
  28.1 52.9 %all-gather.3.cloned.1.call-done = bf16[256,2048]{1,0:T(8,128)(2,1)} async-done(((bf16[256,128]{1,0:T(8,128)(2,1)}), bf16[256,2048]{1,0:T(8,128)(2,1)}) %all-gather.3.cloned.1.call-update) | async-done | bytes 1048592 | tf_op jit(solution)/shard_map/all_gather | solution.py:193
  81.0 97.0 %all-gather.5.cloned.1.call-done = bf16[2048,1024]{1,0:T(8,128)(2,1)} async-done(((bf16[256,1024]{1,0:T(8,128)(2,1)}), bf16[2048,1024]{1,0:T(8,128)(2,1)}) %all-gather.5.cloned.1.call-update) | async-done | bytes 4194320 | tf_op jit(solution)/shard_map/all_gather | solution.py:194
  178.0 4.7 %fusion.34 = f32[256,1024]{1,0:T(8,128)} fusion(bf16[256,2048]{1,0:T(8,128)(2,1)} %all-gather.3.cloned.1.call-done, bf16[2048,1024]{1,0:T(8,128)(2,1)} %all-gather.5.cloned.1.call-done), kind=kOutput, calls=%fused_computation.82 | convolution fusion | flops 1073741824 | bytes 6291456 | tf_op jit(solution)/shard_map/dot_general | solution.py:195
  184.8 2.2 collective-permute-start.2
  186.9 6.7 %collective-permute-start.3 = (f32[1,4]{1,0:T(1,128)S(1)}, f32[1,4]{1,0:T(1,128)S(1)}, u32[]{:S(2)}, u32[]{:S(2)}) collective-permute-start(f32[1,4]{1,0:T(1,128)S(1)} %pad_maximum_fusion.1), channel_id=1, source_target_pairs={{64,0},{128,64},{192,128},{256,192},{320,256},{384,320},{448,384},... | collective-permute-start | bytes 56 | tf_op jit(solution)/shard_map/ppermute | solution.py:139
  195.2 3.2 %collective-permute-start.4 = (f32[3,4]{1,0:T(4,128)S(1)}, f32[3,4]{1,0:T(4,128)S(1)}, u32[]{:S(2)}, u32[]{:S(2)}) collective-permute-start(f32[3,4]{1,0:T(4,128)S(1)} %pad_maximum_fusion), channel_id=1, source_target_pairs={{0,4},{4,8},{8,12},{12,16},{16,20},{20,24},{24,28},{28,32},{32,36}... | collective-permute-start | bytes 152 | tf_op jit(solution)/shard_map/ppermute | solution.py:138
  198.4 4.4 %collective-permute-start.5 = (f32[3,4]{1,0:T(4,128)S(1)}, f32[3,4]{1,0:T(4,128)S(1)}, u32[]{:S(2)}, u32[]{:S(2)}) collective-permute-start(f32[3,4]{1,0:T(4,128)S(1)} %pad_maximum_fusion), channel_id=1, source_target_pairs={{4,0},{8,4},{12,8},{16,12},{20,16},{24,20},{28,24},{32,28},{36,32}... | collective-permute-start | bytes 152 | tf_op jit(solution)/shard_map/ppermute | solution.py:139
  203.7 5.4 %collective-permute-start.6 = (f32[9,4]{0,1:T(4,128)S(1)}, f32[9,4]{0,1:T(4,128)S(1)}, u32[]{:S(2)}, u32[]{:S(2)}) collective-permute-start(f32[9,4]{0,1:T(4,128)S(1)} %concatenate.16), channel_id=1, source_target_pairs={{0,1},{1,2},{2,3},{3,0},{4,5},{5,6},{6,7},{7,4},{8,9},{9,10},{10,1... | collective-permute-start | bytes 440 | tf_op jit(solution)/shard_map/ppermute | solution.py:138
  209.1 1.9 collective-permute-start.7
  211.0 2.9 %collective-permute-done.7 = f32[9,4]{0,1:T(4,128)S(1)} collective-permute-done((f32[9,4]{0,1:T(4,128)S(1)}, f32[9,4]{0,1:T(4,128)S(1)}, u32[]{:S(2)}, u32[]{:S(2)}) %collective-permute-start.7) | collective-permute-done | bytes 176 | tf_op jit(solution)/shard_map/ppermute | solution.py:139
  214.1 1.7 select_reduce_fusion.1
  215.8 0.7 select_reduce_fusion
  216.6 24.0 %shard_map.86 = f32[4,128]{1,0:T(4,128)} custom-call(f32[4,128]{1,0:T(4,128)} %bitcast.42), custom_call_target="tpu_custom_call" | custom-call | tf_op jit(solution)/shard_map/pallas_call | solution.py:117
  240.5 0.8 select_reduce_fusion.2
  241.4 1.4 fusion.1
  (46 shorter events, 5.0 us)
Async XLA Ops:
  7.2 73.9 %all-gather.3.cloned.1.call-start = ((), (), s32[]{:S(2)}) async-start(), calls=%async_computation.1 | async-start | bytes 1114112 | tf_op jit(solution)/shard_map/all_gather | solution.py:193
  9.1 5.3 %collective-permute-start = (bf16[256,128]{1,0:T(8,128)(2,1)S(1)}, bf16[256,128]{1,0:T(8,128)(2,1)S(1)}, u32[]{:S(2)}, u32[]{:S(2)}) collective-permute-start(bf16[256,128]{1,0:T(8,128)(2,1)S(1)} %slice.45), channel_id=1, source_target_pairs={{0,2},{1,3},{4,6},{5,7},{8,10},{9,11},{12,14},{13,15},{16,18},{17,... | collective-permute-start | bytes 196616 | tf_op jit(solution)/shard_map/ppermute | solution.py:190
  15.0 163.0 %all-gather.5.cloned.1.call-start = ((), (), s32[]{:S(2)}) async-start(), calls=%async_computation.2 | async-start | bytes 4718592 | tf_op jit(solution)/shard_map/all_gather | solution.py:194
  17.3 9.8 %collective-permute-start.1 = (bf16[2,128,1024]{2,1,0:T(8,128)(2,1)S(1)}, bf16[2,128,1024]{2,1,0:T(8,128)(2,1)S(1)}, u32[]{:S(2)}, u32[]{:S(2)}) collective-permute-start(bf16[2,128,1024]{2,1,0:T(8,128)(2,1)S(1)} %slice_bitcast_fusion), channel_id=1, source_target_pairs={{0,2},{1,3},{4,6},{5,7},{8,10},{9,11},{12,14},{13,15},{16,18},{17,... | collective-permute-start | bytes 1572872 | tf_op jit(solution)/shard_map/ppermute | solution.py:189
  28.0 155.4 %copy-start.2 = (f32[5]{0:T(128)S(1)}, f32[5]{0:T(128)}, u32[]{:S(2)}) copy-start(f32[5]{0:T(128)} %param.13) | copy-start | bytes 64
  28.0 156.0 %copy-start.1 = (f32[3,1]{0,1:T(1,128)S(1)}, f32[3,1]{0,1:T(1,128)}, u32[]{:S(2)}) copy-start(f32[3,1]{0,1:T(1,128)} %param.12) | copy-start | bytes 40
  28.0 165.7 %copy-start = (s32[512]{0:T(512)S(1)}, s32[512]{0:T(512)}, u32[]{:S(2)}) copy-start(s32[512]{0:T(512)} %param.10) | copy-start | bytes 6148
  28.0 186.0 %reduce-scatter.2.cloned.1.call-start = ((), (), s32[]{:S(2)}) async-start(), calls=%async_computation.3 | async-start | bytes 1310720 | tf_op jit(solution)/shard_map/reduce_scatter | solution.py:196
  184.8 9.7 %collective-permute-start.2 = (f32[1,4]{1,0:T(1,128)S(1)}, f32[1,4]{1,0:T(1,128)S(1)}, u32[]{:S(2)}, u32[]{:S(2)}) collective-permute-start(f32[1,4]{1,0:T(1,128)S(1)} %pad_maximum_fusion.1), channel_id=1, source_target_pairs={{0,64},{64,128},{128,192},{192,256},{256,320},{320,384},{384,448},... | collective-permute-start | bytes 56 | tf_op jit(solution)/shard_map/ppermute | solution.py:138
  186.9 7.5 %collective-permute-start.3 = (f32[1,4]{1,0:T(1,128)S(1)}, f32[1,4]{1,0:T(1,128)S(1)}, u32[]{:S(2)}, u32[]{:S(2)}) collective-permute-start(f32[1,4]{1,0:T(1,128)S(1)} %pad_maximum_fusion.1), channel_id=1, source_target_pairs={{64,0},{128,64},{192,128},{256,192},{320,256},{384,320},{448,384},... | collective-permute-start | bytes 56 | tf_op jit(solution)/shard_map/ppermute | solution.py:139
  195.2 7.8 %collective-permute-start.4 = (f32[3,4]{1,0:T(4,128)S(1)}, f32[3,4]{1,0:T(4,128)S(1)}, u32[]{:S(2)}, u32[]{:S(2)}) collective-permute-start(f32[3,4]{1,0:T(4,128)S(1)} %pad_maximum_fusion), channel_id=1, source_target_pairs={{0,4},{4,8},{8,12},{12,16},{16,20},{20,24},{24,28},{28,32},{32,36}... | collective-permute-start | bytes 152 | tf_op jit(solution)/shard_map/ppermute | solution.py:138
  198.4 5.1 %collective-permute-start.5 = (f32[3,4]{1,0:T(4,128)S(1)}, f32[3,4]{1,0:T(4,128)S(1)}, u32[]{:S(2)}, u32[]{:S(2)}) collective-permute-start(f32[3,4]{1,0:T(4,128)S(1)} %pad_maximum_fusion), channel_id=1, source_target_pairs={{4,0},{8,4},{12,8},{16,12},{20,16},{24,20},{28,24},{32,28},{36,32}... | collective-permute-start | bytes 152 | tf_op jit(solution)/shard_map/ppermute | solution.py:139
  203.7 7.3 %collective-permute-start.6 = (f32[9,4]{0,1:T(4,128)S(1)}, f32[9,4]{0,1:T(4,128)S(1)}, u32[]{:S(2)}, u32[]{:S(2)}) collective-permute-start(f32[9,4]{0,1:T(4,128)S(1)} %concatenate.16), channel_id=1, source_target_pairs={{0,1},{1,2},{2,3},{3,0},{4,5},{5,6},{6,7},{7,4},{8,9},{9,10},{10,1... | collective-permute-start | bytes 440 | tf_op jit(solution)/shard_map/ppermute | solution.py:138
  209.1 4.9 %collective-permute-start.7 = (f32[9,4]{0,1:T(4,128)S(1)}, f32[9,4]{0,1:T(4,128)S(1)}, u32[]{:S(2)}, u32[]{:S(2)}) collective-permute-start(f32[9,4]{0,1:T(4,128)S(1)} %concatenate.16), channel_id=1, source_target_pairs={{1,0},{2,1},{3,2},{0,3},{5,4},{6,5},{7,6},{4,7},{9,8},{10,9},{11,1... | collective-permute-start | bytes 440 | tf_op jit(solution)/shard_map/ppermute | solution.py:139
Sparse Core Ops, SparseCore 0:
  15.1 65.8 all-gather.2
  84.8 93.1 all-gather.4
  182.9 27.1 reduce-scatter.1

commit v2 on v1

--- a/solution.py
+++ b/solution.py
@@ -131,13 +131,314 @@
     )(part)
 
 
-def with_neighbours(block, axis):
-    count = lax.axis_size(axis)
-    upward = [(i, (i + 1) % count) for i in range(count)]
-    downward = [(target, source) for source, target in upward]
-    below = lax.ppermute(block, axis, upward)
-    above = lax.ppermute(block, axis, downward)
-    return jnp.concatenate([below, block, above], axis=0)
+REACH = 32
+
+
+def wanted_cols(window_blocks, col_blocks):
+    return (window_blocks + 2 * REACH + col_blocks - 1) // col_blocks
+
+
+def gather_kernel(
+    density_ref, margin_ref, near_ref, product_ref, near_out,
+    dens, marg, around,
+    sem_around, got_around, sem_piece, sem_ring, sem_pair, got_slab, got_pair,
+    sem_strip, sem_y, sem_half, got_strip, got_half,
+):
+    row = lax.axis_index("row")
+    col = lax.axis_index("col")
+    layer = lax.axis_index("layer")
+    n_row = lax.axis_size("row")
+    n_col = lax.axis_size("col")
+    n_layer = lax.axis_size("layer")
+    share, strip = marg.shape[1], marg.shape[2]
+    slab = dens.shape[1] // 2
+    y, x = row // 2, row % 2
+    part = layer % 2
+    live = col < wanted_cols(n_row * dens.shape[1] // BLK, margin_ref.shape[1] // BLK)
+    rows_of = (n_row, marg.shape[0] - n_row)
+    cols_of = (n_col, dens.shape[0] - n_col)
+
+    def remote(source, target, sent, got, device):
+        return pltpu.make_async_remote_copy(
+            src_ref=source, dst_ref=target, send_sem=sent, recv_sem=got,
+            device_id=device, device_id_type=MESH,
+        )
+
+    def when(condition, body):
+        pl.when(condition)(body)
+
+    shifts = [
+        (dr, dc, dl) for dl in (-1, 0, 1) for dc in (-1, 0, 1) for dr in (-1, 0, 1)
+    ]
+    plane = [(xx, ll) for ll in range(n_layer) for xx in range(2)]
+    up, down = ((row + 2) % n_row, col, layer), ((row + n_row - 2) % n_row, col, layer)
+    onward, back = (row, (col + 1) % n_col, layer), (row, (col + n_col - 1) % n_col, layer)
+    partner = (row, col, layer + 1 - 2 * part)
+
+    def shifted(shift):
+        return (
+            (row + shift[0] + n_row) % n_row,
+            (col + shift[1] + n_col) % n_col,
+            (layer + shift[2] + n_layer) % n_layer,
+        )
+
+    barrier = pltpu.get_barrier_semaphore()
+    for shift in shifts:
+        if shift != (0, 0, 0):
+            pl.semaphore_signal(barrier, inc=1, device_id=shifted(shift), device_id_type=MESH)
+    for device in (up, down):
+        pl.semaphore_signal(barrier, inc=1, device_id=device, device_id_type=MESH)
+    for xx in range(2):
+        for step in range(n_layer):
+            if (xx, step) != (0, 0):
+                device = (2 * y + (x + xx) % 2, col, (layer + step) % n_layer)
+                pl.semaphore_signal(barrier, inc=1, device_id=device, device_id_type=MESH)
+    pl.semaphore_wait(barrier, 26 + 2 + 7)
+
+    def piece_copy(kind, target_layer, start):
+        slot = dens.at[kind * n_col + col, pl.ds(slab * (target_layer % 2), slab)]
+        source = density_ref.at[pl.ds(slab * (target_layer % 2), slab)]
+        sent, got = sem_piece.at[target_layer], got_slab.at[kind * n_col + col]
+        here = layer == target_layer
+        far = remote(source, slot, sent, got, (row, col, target_layer))
+        if start:
+            when(here, pltpu.make_async_copy(source, slot, got).start)
+        when(jnp.logical_not(here), far.start if start else far.wait_send)
+
+    def strip_copy(kind, target, start):
+        xx, ll = target
+        slot = marg.at[kind * n_row + row]
+        source = margin_ref.at[:, pl.ds(strip * ll, strip)]
+        sent, got = sem_strip.at[ll * 2 + xx], got_strip.at[kind * n_row + row]
+        here = (layer == ll) & (x == xx)
+        far = remote(source, slot, sent, got, (2 * y + xx, col, ll))
+        if start:
+            when(here, pltpu.make_async_copy(source, slot, got).start)
+        when(jnp.logical_not(here), far.start if start else far.wait_send)
+
+    def first_copies(start):
+        for kind in range(2):
+
+            def pieces(kind=kind):
+                for ll in range(n_layer):
+                    piece_copy(kind, ll, start)
+
+            def strips(kind=kind):
+                for target in plane:
+                    strip_copy(kind, target, start)
+
+            when((layer == kind) & (col < cols_of[kind]), pieces)
+            when((layer == kind) & (row < rows_of[kind]) & live, strips)
+
+    def around_copy(index):
+        dr, dc, dl = shifts[index]
+        return remote(
+            near_ref, around.at[26 - index], sem_around.at[index], got_around.at[26 - index],
+            shifted(shifts[index]),
+        )
+
+    def slab_of(kind, origin, half):
+        return dens.at[kind * n_col + origin, pl.ds(pl.multiple_of(slab * half, slab), slab)]
+
+    def ring_copy(kind, origin, way, step):
+        block = slab_of(kind, origin, part)
+        return remote(
+            block, block, sem_ring.at[kind, way, step], got_slab.at[kind * n_col + origin],
+            (onward, back)[way],
+        )
+
+    def pair_copy(kind, origin):
+        block = slab_of(kind, origin, part)
+        return remote(
+            block, block, sem_pair.at[kind * n_col + origin],
+            got_pair.at[kind * n_col + origin], partner,
+        )
+
+    def pair_wait(kind, origin):
+        block = slab_of(kind, origin, 1 - part)
+        remote(
+            block, block, sem_pair.at[kind * n_col + origin],
+            got_pair.at[kind * n_col + origin], partner,
+        ).wait_recv()
+
+    def ring_step(step, start):
+        half = n_col // 2
+        for way in ((0, 1) if step and step < half else (0,)):
+            origin = (col + (n_col - step if way == 0 else step)) % n_col
+            for kind in range(2):
+
+                def body(kind=kind, origin=origin, way=way):
+                    if start:
+                        ring_copy(kind, origin, way, 0).wait_recv()
+                    sends = [pair_copy(kind, origin)]
+                    if way == 0 and step < half:
+                        sends.append(ring_copy(kind, origin, 0, step))
+                    if step == 0 or (way == 1 and step < half - 1):
+                        sends.append(ring_copy(kind, origin, 1, step))
+                    for copy in reversed(sends):
+                        if start:
+                            copy.start()
+                        else:
+                            copy.wait_send()
+
+                when(origin < cols_of[kind], body)
+
+    def own_strip(kind, other, start):
+        origin = 2 * y + (x + other) % 2
+        block = marg.at[kind * n_row + origin]
+        got = got_strip.at[kind * n_row + origin]
+
+        def body():
+            copies = [
+                remote(block, block, sem_y.at[kind, other, way], got, (up, down)[way])
+                for way in range(2)
+            ]
+            if start:
+                copies[0].wait_recv()
+            for copy in copies:
+                if start:
+                    copy.start()
+                else:
+                    copy.wait_send()
+
+        when(live & (origin < rows_of[kind]), body)
+
+    def next_strip(kind, xx, way, start):
+        origin = 2 * ((y + (3 if way == 0 else 1)) % 4) + xx
+        whole = marg.at[kind * n_row + origin]
+        block = marg.at[kind * n_row + origin, pl.ds(share // 2 * way, share // 2)]
+
+        def body():
+            if start:
+                remote(
+                    whole, whole, sem_y.at[kind, xx, way], got_strip.at[kind * n_row + origin], up
+                ).wait_recv()
+            copy = remote(
+                block, block, sem_half.at[kind, xx, way],
+                got_half.at[kind * n_row + origin, way], (up, down)[way],
+            )
+            if start:
+                copy.start()
+            else:
+                copy.wait_send()
+
+        when(live & (origin < rows_of[kind]), body)
+
+    def far_strip(kind, xx):
+        origin = 2 * ((y + 2) % 4) + xx
+
+        def body():
+            for way in range(2):
+                block = marg.at[kind * n_row + origin, pl.ds(share // 2 * way, share // 2)]
+                remote(
+                    block, block, sem_half.at[kind, xx, way],
+                    got_half.at[kind * n_row + origin, way], up,
+                ).wait_recv()
+
+        when(live & (origin < rows_of[kind]), body)
+
+    def relays(start):
+        ring_step(0, start)
+        own_strip(0, 0, start)
+        ring_step(1, start)
+        own_strip(1, 0, start)
+        ring_step(2, start)
+        ring_step(3, start)
+        own_strip(0, 1, start)
+        ring_step(4, start)
+        ring_step(5, start)
+        own_strip(1, 1, start)
+        ring_step(6, start)
+        for way in range(2):
+            for xx in range(2):
+                next_strip(0, xx, way, start)
+        ring_step(7, start)
+        for way in range(2):
+            for xx in range(2):
+                next_strip(1, xx, way, start)
+        ring_step(8, start)
+
+    first_copies(True)
+    for index in range(27):
+        if index != 13:
+            around_copy(index).start()
+    relays(True)
+    for kind in range(2):
+        for origin in range(cols_of[kind]):
+            pair_wait(kind, origin)
+        for xx in range(2):
+            far_strip(kind, xx)
+
+    @pl.when(live)
+    def _():
+        product_ref[...] = jnp.zeros_like(product_ref)
+
+        def add_share(j, carry):
+            for side in range(2):
+                product_ref[...] += jnp.dot(
+                    dens[2 * j + side],
+                    marg[j, pl.ds(share // 2 * side, share // 2)],
+                    preferred_element_type=jnp.float32,
+                )
+            return carry
+
+        lax.fori_loop(0, marg.shape[0], add_share, 0)
+
+    @pl.when(jnp.logical_not(live))
+    def _():
+        product_ref[...] = jnp.zeros_like(product_ref)
+
+    for index in range(27):
+        if index != 13:
+            around_copy(26 - index).wait_recv()
+            near_out[index] = around[index]
+    near_out[13] = near_ref[...]
+    first_copies(False)
+    for index in range(27):
+        if index != 13:
+            around_copy(index).wait_send()
+    relays(False)
+
+
+def gather_product(density, margin, near):
+    rows_here, piece_width = density.shape
+    share, share_cols = margin.shape
+    n_row, n_col, n_layer = (lax.axis_size(axis) for axis in ("row", "col", "layer"))
+    depth = n_row * rows_here + REACH * BLK
+    strip = share_cols // n_layer
+    dma = pltpu.SemaphoreType.DMA
+    vmem = pl.BlockSpec(memory_space=pltpu.VMEM)
+    anywhere = pl.BlockSpec(memory_space=pl.ANY)
+    pieces, shares = depth // piece_width, depth // share
+    return pl.pallas_call(
+        gather_kernel,
+        out_shape=(
+            jax.ShapeDtypeStruct((rows_here, strip), jnp.float32),
+            jax.ShapeDtypeStruct((27,) + near.shape, jnp.float32),
+        ),
+        in_specs=[anywhere, anywhere, vmem],
+        out_specs=(vmem, vmem),
+        scratch_shapes=[
+            pltpu.VMEM((pieces, rows_here, piece_width), jnp.bfloat16),
+            pltpu.VMEM((shares, share, strip), jnp.bfloat16),
+            pltpu.VMEM((27,) + near.shape, jnp.float32),
+            dma((27,)),
+            dma((27,)),
+            dma((n_layer,)),
+            dma((2, 2, n_col // 2)),
+            dma((pieces,)),
+            dma((pieces,)),
+            dma((pieces,)),
+            dma((2 * n_layer,)),
+            dma((2, 2, 2)),
+            dma((2, 2, 2)),
+            dma((shares,)),
+            dma((shares, 2)),
+        ],
+        compiler_params=pltpu.CompilerParams(
+            collective_id=1, has_side_effects=True, vmem_limit_bytes=24 * 1024 * 1024
+        ),
+    )(density, margin, near)
 
 
 def near_profile(cells, tile_of, extent, offset, exponent_of):
@@ -168,9 +469,8 @@
     col_index = lax.axis_index("col")
     layer_index = lax.axis_index("layer")
     exponent_here = kind_exponent(atom_kind, exponents)
-    near = jnp.concatenate([exponent_here[:, None], atom_offset.T], axis=1)
-    for axis in ("row", "col", "layer"):
-        near = with_neighbours(near, axis)
+    near_here = jnp.concatenate([exponent_here[:, None], atom_offset.T], axis=1)
+    near_here = jnp.broadcast_to(jnp.pad(near_here, ((0, 0), (0, 124))), (8, 128))
     density_mask = lax.dynamic_slice(
         block_pattern,
         (row_index * (rows_here // BLK), (layer_index * n_col + col_index) * piece_width // BLK),
@@ -183,17 +483,8 @@
         (share_rows // BLK, share_cols // BLK),
     )
     margin_masked = apply_pattern(margin, margin_mask)
-    paired_rows = margin_masked.reshape(share_rows // (2 * BLK), 2, BLK, share_cols)
-    lend = [(0, 2), (1, 3)]
-    lender = layer_index < 2
-    margin_lent = lax.ppermute(paired_rows[:, 1], "layer", lend)
-    density_lent = lax.ppermute(masked[:, BLK:], "layer", lend)
-    margin_half = jnp.where(lender, paired_rows[:, 0], margin_lent).reshape(-1, share_cols)
-    density_half = jnp.where(lender, masked[:, :BLK], density_lent)
-    density_all = lax.all_gather(density_half, "col", axis=1, tiled=True)
-    margin_all = lax.all_gather(margin_half, "row", axis=0, tiled=True)
-    product_acc = jnp.dot(density_all, margin_all, preferred_element_type=jnp.float32)
-    product = lax.psum_scatter(product_acc, "layer", scatter_dimension=1, tiled=True)
+    product, near_all = gather_product(masked, margin_masked, near_here)
+    near = near_all[:, 0, :4]
     strip_width = product.shape[1]
     rows_global = row_index * rows_here + jnp.arange(rows_here, dtype=jnp.int32)
     cols_global = (col_index * n_layer + layer_index) * strip_width + jnp.arange(

time: 250 us -> 107 us (0.43)
  waiting for transfers between devices: 161 us -> 0 us
  Pallas kernels: 24 us -> 95.3 us
  starting transfers between devices: 31.5 us -> 0 us
  between operations: 14.7 us -> 1.47 us
  other arithmetic: 11.2 us -> 5.28 us
  matrix products: 6.16 us -> 1.43 us
    all_gather x2 -> x0, waiting for transfers between devices: 150 us -> none  [the longest x1 97 us: shards(): margin_all = lax.all_gather(margin_half, 'row', axis=0, tiled=True)]
    pallas_call x0 -> x1, Pallas kernels: none -> 54.8 us  [gather_product(): pl.pallas_call(gather_kernel, out_shape=(jax.ShapeDtypeStruct((rows_here,...]
    ppermute x8 -> x0, starting transfers between devices: 31.4 us -> none  [the longest x3 13 us: with_neighbours(): above = lax.ppermute(block, axis, downward)]
    pallas_call x1, Pallas kernels: 24 us -> 40.5 us  [spread(): pl.pallas_call(spread_kernel, out_shape=jax.ShapeDtypeStruct(part.shape,...]
    ppermute x8 -> x0, waiting for transfers between devices: 10.8 us -> none  [the longest x1 6.08 us: shards(): margin_lent = lax.ppermute(paired_rows[:, 1], 'layer', lend)]
    dot_general x1 -> x0, matrix products: 4.73 us -> none  [shards(): jnp.dot(density_all, margin_all, preferred_element_type=jnp.float32)]
    unnamed x6 -> x12, local copies, waits for them, and re-layouts: 0.02 us -> 2.76 us
  transfers between devices with their start and end apart: 11 -> 0, of which waited for: 6 -> 0; matrix products, arithmetic and copies ran while one was open for 3% -> 0% of each run, Pallas kernels for 0% -> 0%
where the time goes in v2:
time: 107 us
  Pallas kernels  95.3 us (89%)
  other arithmetic  5.28 us (5%)
  local copies, waits for them, and re-layouts  3.4 us (3%)
  between operations  1.47 us (1%)
  matrix products  1.43 us (1%)
    pallas_call x1, Pallas kernels, gather_product(): pl.pallas_call(gather_kernel, out_shape=(jax.ShapeDtypeStruct((rows_here,...  54.8 us
    pallas_call x1, Pallas kernels, spread(): pl.pallas_call(spread_kernel, out_shape=jax.ShapeDtypeStruct(part.shape,...  40.5 us
    unnamed x12, local copies, waits for them, and re-layouts  2.76 us

profile of v2, /device:TPU:1, one launch (start us, length us, event | category | flops | bytes accessed | tf_op | source)
XLA Modules:
  0.0 106.9 jit_solution(3033409830789128014)
XLA Ops:
  0.7 0.9 dynamic-slice_convert_fusion
  1.5 0.2 mul.168
  1.8 0.1 copy-done
  1.9 0.1 bitcast_multiply_fusion.margin_ref
  2.0 0.0 copy-start.1
  2.1 0.8 dynamic-slice_convert_fusion.1
  2.9 0.1 mul.162
  3.7 0.6 copy-done.4
  4.3 0.6 fusion.25
  4.9 0.7 copy-done.5
  5.6 0.7 fusion.31
  6.3 54.8 %shard_map.86 = (f32[256,256]{1,0:T(8,128)S(1)}, f32[27,8,128]{2,1,0:T(8,128)S(1)}) custom-call(bf16[256,256]{1,0:T(8,128)(2,1)S(1)} %bitcast_multiply_fusion.1.density_ref, bf16[512,1024]{1,0:T(8,128)(2,1)S(1)} %bitcast_multiply_fusion.margin_ref, f32[8,128]{1,0:T(8,128)S(1)} %broadcast_in_dim.79.near_ref), custom_call_target="tpu_custom_call" | custom-call | tf_op jit(solution)/shard_map/pallas_call | solution.py:413
  61.2 0.7 select_reduce_fusion.1
  61.9 0.7 copy-done.2
  62.5 0.3 reduce-window.9
  62.8 0.1 slice.24
  63.0 0.1 slice_reduce_fusion
  63.1 0.1 fusion.34
  63.2 0.8 select_reduce_fusion
  63.9 40.5 %shard_map.87 = f32[4,128]{1,0:T(4,128)} custom-call(f32[4,128]{1,0:T(4,128)} %bitcast.36), custom_call_target="tpu_custom_call" | custom-call | tf_op jit(solution)/shard_map/pallas_call | solution.py:117
  104.4 0.6 copy-done.3
  105.1 0.2 select_reduce_fusion.2
  105.3 0.1 copy.11
  105.4 1.4 %fusion = f32[32,32,128]{2,1,0:T(8,128)} fusion(f32[27,32]{0,1:T(8,128)S(1)} %get-tuple-element.15, f32[27,32]{0,1:T(8,128)S(1)} %get-tuple-element.14, f32[27]{0:T(128)S(1)} %get-tuple-element.12, f32[27]{0:T(128)S(1)} %get-tuple-element.10, s32[27]{0:T(128)S(1)} %add_multiply_fusion), kind=kOutput, calls=%fused_computation.1 | convolution fusion | flops 42522624 | bytes 531524 | tf_op jit(solution)/shard_map/axy,az->xyz/dot_general | solution.py:459
  (16 shorter events, 0.2 us)
Async XLA Ops:
  0.6 1.2 %copy-start = (bf16[512,1024]{1,0:T(8,128)(2,1)S(1)}, bf16[512,1024]{1,0:T(8,128)(2,1)}, u32[]{:S(2)}) copy-start(bf16[512,1024]{1,0:T(8,128)(2,1)} %param.8) | copy-start | bytes 3145732
  2.0 1.0 copy-start.1
  3.7 0.7 copy-start.4
  4.9 0.7 copy-start.5
  61.9 0.7 copy-start.2
  104.4 0.7 copy-start.3

commit v3 on v2

--- a/solution.py
+++ b/solution.py
@@ -14,123 +14,6 @@
 MESH = pl.DeviceIdType.MESH
 
 
-def spread_kernel(part_ref, out_ref, mine, slots, send_a, recv_a, send_b, recv_b):
-    row = lax.axis_index("row")
-    col = lax.axis_index("col")
-    layer = lax.axis_index("layer")
-    n_row = slots.shape[0]
-    n_layer = lax.axis_size("layer")
-    others = lax.axis_size("col") * n_layer
-    home_col = row // n_layer
-    home_layer = row % n_layer
-    home = (col == home_col) & (layer == home_layer)
-    barrier = pltpu.get_barrier_semaphore()
-
-    @pl.when(jnp.logical_not(home))
-    def _():
-        pl.semaphore_signal(
-            barrier, inc=1, device_id=(row, home_col, home_layer), device_id_type=MESH
-        )
-
-    for step in range(1, n_row):
-        mate = (row + step) % n_row
-        pl.semaphore_signal(barrier, inc=1, device_id=(mate, col, layer), device_id_type=MESH)
-
-    def copy_a(index):
-        return pltpu.make_async_remote_copy(
-            src_ref=part_ref,
-            dst_ref=mine,
-            send_sem=send_a.at[index],
-            recv_sem=recv_a,
-            device_id=(row, index // n_layer, index % n_layer),
-            device_id_type=MESH,
-        )
-
-    def copies_b(source):
-        return [
-            pltpu.make_async_remote_copy(
-                src_ref=source,
-                dst_ref=slots.at[row],
-                send_sem=send_b.at[step],
-                recv_sem=recv_b.at[row],
-                device_id=((row + step) % n_row, col, layer),
-                device_id_type=MESH,
-            )
-            for step in range(1, n_row)
-        ]
-
-    @pl.when(home)
-    def _():
-        pl.semaphore_wait(barrier, others - 1 + n_row - 1)
-        for copy in copies_b(part_ref):
-            copy.start()
-        own = col * n_layer + layer
-
-        def send_one(step, carry):
-            copy_a((own + step) % others).start()
-            return carry
-
-        def end_one(step, carry):
-            copy_a((own + step) % others).wait_send()
-            return carry
-
-        lax.fori_loop(1, others, send_one, 0)
-        lax.fori_loop(1, others, end_one, 0)
-        for copy in copies_b(part_ref):
-            copy.wait_send()
-
-    @pl.when(jnp.logical_not(home))
-    def _():
-        pl.semaphore_wait(barrier, n_row - 1)
-        copy_a(0).wait_recv()
-        for copy in copies_b(mine):
-            copy.start()
-        for copy in copies_b(mine):
-            copy.wait_send()
-
-    for step in range(1, n_row):
-        mate = (row + step) % n_row
-        pltpu.make_async_remote_copy(
-            src_ref=part_ref,
-            dst_ref=slots.at[mate],
-            send_sem=send_b.at[0],
-            recv_sem=recv_b.at[mate],
-            device_id=(mate, col, layer),
-            device_id_type=MESH,
-        ).wait_recv()
-
-    @pl.when(home)
-    def _():
-        out_ref[...] = part_ref[...]
-
-    @pl.when(jnp.logical_not(home))
-    def _():
-        out_ref[...] = mine[...]
-
-    for step in range(1, n_row):
-        out_ref[...] += slots[(row + step) % n_row]
-
-
-def spread(part):
-    n_row = lax.axis_size("row")
-    others = lax.axis_size("col") * lax.axis_size("layer")
-    return pl.pallas_call(
-        spread_kernel,
-        out_shape=jax.ShapeDtypeStruct(part.shape, part.dtype),
-        in_specs=[pl.BlockSpec(memory_space=pltpu.VMEM)],
-        out_specs=pl.BlockSpec(memory_space=pltpu.VMEM),
-        scratch_shapes=[
-            pltpu.VMEM(part.shape, part.dtype),
-            pltpu.VMEM((n_row,) + part.shape, part.dtype),
-            pltpu.SemaphoreType.DMA((others,)),
-            pltpu.SemaphoreType.DMA,
-            pltpu.SemaphoreType.DMA((n_row,)),
-            pltpu.SemaphoreType.DMA((n_row,)),
-        ],
-        compiler_params=pltpu.CompilerParams(collective_id=0, has_side_effects=True),
-    )(part)
-
-
 REACH = 32
 
 
@@ -139,9 +22,9 @@
 
 
 def gather_kernel(
-    density_ref, margin_ref, near_ref, product_ref, near_out,
-    dens, marg, around,
-    sem_around, got_around, sem_piece, sem_ring, sem_pair, got_slab, got_pair,
+    density_ref, margin_ref, near_ref, bounds_ref, product_ref, near_out, pops_out,
+    dens, marg, around, pops_home, pops_mine, pops_rows,
+    sem_spread, got_mine, sem_rows, got_rows, sem_around, got_around, sem_piece, sem_ring, sem_pair, got_slab, got_pair,
     sem_strip, sem_y, sem_half, got_strip, got_half,
 ):
     row = lax.axis_index("row")
@@ -170,7 +53,10 @@
     shifts = [
         (dr, dc, dl) for dl in (-1, 0, 1) for dc in (-1, 0, 1) for dr in (-1, 0, 1)
     ]
-    plane = [(xx, ll) for ll in range(n_layer) for xx in range(2)]
+    plane = [(0, 2), (1, 2), (0, 3), (1, 3), (0, 0), (0, 1), (1, 0), (1, 1)]
+    home_col, home_layer = row // n_layer, row % n_layer
+    home = (col == home_col) & (layer == home_layer)
+    members = n_col * n_layer
     up, down = ((row + 2) % n_row, col, layer), ((row + n_row - 2) % n_row, col, layer)
     onward, back = (row, (col + 1) % n_col, layer), (row, (col + n_col - 1) % n_col, layer)
     partner = (row, col, layer + 1 - 2 * part)
@@ -193,7 +79,19 @@
             if (xx, step) != (0, 0):
                 device = (2 * y + (x + xx) % 2, col, (layer + step) % n_layer)
                 pl.semaphore_signal(barrier, inc=1, device_id=device, device_id_type=MESH)
-    pl.semaphore_wait(barrier, 26 + 2 + 7)
+    for step in range(1, n_row):
+        device = ((row + step) % n_row, col, layer)
+        pl.semaphore_signal(barrier, inc=1, device_id=device, device_id_type=MESH)
+
+    @pl.when(home)
+    def _():
+        pl.semaphore_wait(barrier, 26 + 2 + 7 + n_row - 1 + members - 1)
+
+    @pl.when(jnp.logical_not(home))
+    def _():
+        device = (row, home_col, home_layer)
+        pl.semaphore_signal(barrier, inc=1, device_id=device, device_id_type=MESH)
+        pl.semaphore_wait(barrier, 26 + 2 + 7 + n_row - 1)
 
     def piece_copy(kind, target_layer, start):
         slot = dens.at[kind * n_col + col, pl.ds(slab * (target_layer % 2), slab)]
@@ -206,13 +104,14 @@
         when(jnp.logical_not(here), far.start if start else far.wait_send)
 
     def strip_copy(kind, target, start):
-        xx, ll = target
+        other, ll = target
+        xx = (x + other) % 2
         slot = marg.at[kind * n_row + row]
         source = margin_ref.at[:, pl.ds(strip * ll, strip)]
-        sent, got = sem_strip.at[ll * 2 + xx], got_strip.at[kind * n_row + row]
-        here = (layer == ll) & (x == xx)
+        sent, got = sem_strip.at[ll * 2 + other], got_strip.at[kind * n_row + row]
+        here = (layer == ll) & (other == 0)
         far = remote(source, slot, sent, got, (2 * y + xx, col, ll))
-        if start:
+        if start and other == 0:
             when(here, pltpu.make_async_copy(source, slot, got).start)
         when(jnp.logical_not(here), far.start if start else far.wait_send)
 
@@ -220,7 +119,7 @@
         for kind in range(2):
 
             def pieces(kind=kind):
-                for ll in range(n_layer):
+                for ll in (2, 3, 0, 1):
                     piece_copy(kind, ll, start)
 
             def strips(kind=kind):
@@ -303,18 +202,18 @@
 
         when(live & (origin < rows_of[kind]), body)
 
-    def next_strip(kind, xx, way, start):
-        origin = 2 * ((y + (3 if way == 0 else 1)) % 4) + xx
+    def next_strip(kind, other, way, start):
+        origin = 2 * ((y + (3 if way == 0 else 1)) % 4) + (x + other) % 2
         whole = marg.at[kind * n_row + origin]
         block = marg.at[kind * n_row + origin, pl.ds(share // 2 * way, share // 2)]
 
         def body():
             if start:
                 remote(
-                    whole, whole, sem_y.at[kind, xx, way], got_strip.at[kind * n_row + origin], up
+                    whole, whole, sem_y.at[kind, other, way], got_strip.at[kind * n_row + origin], up
                 ).wait_recv()
             copy = remote(
-                block, block, sem_half.at[kind, xx, way],
+                block, block, sem_half.at[kind, other, way],
                 got_half.at[kind * n_row + origin, way], (up, down)[way],
             )
             if start:
@@ -337,26 +236,77 @@
 
         when(live & (origin < rows_of[kind]), body)
 
-    def relays(start):
+    def nexts(kind, other, start):
+        for way in range(2):
+            next_strip(kind, other, way, start)
+
+    def relays_low(start):
         ring_step(0, start)
         own_strip(0, 0, start)
+        own_strip(1, 0, start)
         ring_step(1, start)
+        ring_step(2, start)
+        nexts(0, 0, start)
+        ring_step(3, start)
+        ring_step(4, start)
+        nexts(1, 0, start)
+        ring_step(5, start)
+        ring_step(6, start)
+        own_strip(0, 1, start)
+        ring_step(7, start)
+        ring_step(8, start)
+        own_strip(1, 1, start)
+        nexts(0, 1, start)
+        nexts(1, 1, start)
+
+    def relays_high(start):
+        ring_step(0, start)
+        ring_step(1, start)
+        own_strip(0, 1, start)
+        ring_step(2, start)
+        own_strip(0, 0, start)
+        ring_step(3, start)
+        own_strip(1, 1, start)
+        ring_step(4, start)
         own_strip(1, 0, start)
-        ring_step(2, start)
-        ring_step(3, start)
-        own_strip(0, 1, start)
-        ring_step(4, start)
         ring_step(5, start)
-        own_strip(1, 1, start)
         ring_step(6, start)
-        for way in range(2):
-            for xx in range(2):
-                next_strip(0, xx, way, start)
+        nexts(0, 1, start)
         ring_step(7, start)
-        for way in range(2):
-            for xx in range(2):
-                next_strip(1, xx, way, start)
+        nexts(0, 0, start)
         ring_step(8, start)
+        nexts(1, 1, start)
+        nexts(1, 0, start)
+
+    def relays(start):
+        when(layer < 2, lambda: relays_low(start))
+        when(layer >= 2, lambda: relays_high(start))
+
+    def spread_copy(index):
+        return remote(
+            pops_home, pops_mine, sem_spread.at[index], got_mine,
+            (row, index // n_layer, index % n_layer),
+        )
+
+    def row_copies(source):
+        return [
+            remote(
+                source, pops_rows.at[row], sem_rows.at[step], got_rows.at[row],
+                ((row + step) % n_row, col, layer),
+            )
+            for step in range(1, n_row)
+        ]
+
+    def spread_step(start):
+        def body(step, carry):
+            copy = spread_copy((col * n_layer + layer + step) % members)
+            if start:
+                copy.start()
+            else:
+                copy.wait_send()
+            return carry
+
+        lax.fori_loop(1, members, body, 0)
 
     first_copies(True)
     for index in range(27):
@@ -388,19 +338,60 @@
     def _():
         product_ref[...] = jnp.zeros_like(product_ref)
 
+    @pl.when(home)
+    def _():
+        side = product_ref.shape
+        here = lax.broadcasted_iota(jnp.int32, side, 0) == lax.broadcasted_iota(jnp.int32, side, 1)
+        diagonal = jnp.sum(jnp.where(here, product_ref[...], 0.0), axis=1, keepdims=True)
+        wide = (side[0], bounds_ref.shape[1])
+        function = lax.broadcasted_iota(jnp.int32, wide, 0) + row * side[0]
+        member = (function >= bounds_ref[0:1, :]) & (function < bounds_ref[1:2, :])
+        pops_home[...] = jnp.sum(jnp.where(member, diagonal, 0.0), axis=0, keepdims=True)
+
     for index in range(27):
         if index != 13:
             around_copy(26 - index).wait_recv()
             near_out[index] = around[index]
     near_out[13] = near_ref[...]
+
+    @pl.when(home)
+    def _():
+        for copy in row_copies(pops_home):
+            copy.start()
+        spread_step(True)
+
+    @pl.when(jnp.logical_not(home))
+    def _():
+        spread_copy(0).wait_recv()
+        for copy in row_copies(pops_mine):
+            copy.start()
+
     first_copies(False)
     for index in range(27):
         if index != 13:
             around_copy(index).wait_send()
     relays(False)
-
-
-def gather_product(density, margin, near):
+    for step in range(1, n_row):
+        mate = (row + step) % n_row
+        slot = pops_rows.at[mate]
+        remote(slot, slot, sem_rows.at[0], got_rows.at[mate], (mate, col, layer)).wait_recv()
+
+    @pl.when(home)
+    def _():
+        pops_out[...] = pops_home[...]
+        spread_step(False)
+
+    @pl.when(jnp.logical_not(home))
+    def _():
+        pops_out[...] = pops_mine[...]
+
+    for step in range(1, n_row):
+        pops_out[...] += pops_rows[(row + step) % n_row]
+    for copy in row_copies(pops_mine):
+        copy.wait_send()
+
+
+def gather_product(density, margin, near, bounds):
     rows_here, piece_width = density.shape
     share, share_cols = margin.shape
     n_row, n_col, n_layer = (lax.axis_size(axis) for axis in ("row", "col", "layer"))
@@ -415,13 +406,21 @@
         out_shape=(
             jax.ShapeDtypeStruct((rows_here, strip), jnp.float32),
             jax.ShapeDtypeStruct((27,) + near.shape, jnp.float32),
+            jax.ShapeDtypeStruct((1, bounds.shape[1]), jnp.float32),
         ),
-        in_specs=[anywhere, anywhere, vmem],
-        out_specs=(vmem, vmem),
+        in_specs=[anywhere, anywhere, vmem, vmem],
+        out_specs=(vmem, vmem, vmem),
         scratch_shapes=[
             pltpu.VMEM((pieces, rows_here, piece_width), jnp.bfloat16),
             pltpu.VMEM((shares, share, strip), jnp.bfloat16),
             pltpu.VMEM((27,) + near.shape, jnp.float32),
+            pltpu.VMEM((1, bounds.shape[1]), jnp.float32),
+            pltpu.VMEM((1, bounds.shape[1]), jnp.float32),
+            pltpu.VMEM((n_row, 1, bounds.shape[1]), jnp.float32),
+            dma((n_col * n_layer,)),
+            dma,
+            dma((n_row,)),
+            dma((n_row,)),
             dma((27,)),
             dma((27,)),
             dma((n_layer,)),
@@ -438,7 +437,7 @@
         compiler_params=pltpu.CompilerParams(
             collective_id=1, has_side_effects=True, vmem_limit_bytes=24 * 1024 * 1024
         ),
-    )(density, margin, near)
+    )(density, margin, near, bounds)
 
 
 def near_profile(cells, tile_of, extent, offset, exponent_of):
@@ -483,22 +482,11 @@
         (share_rows // BLK, share_cols // BLK),
     )
     margin_masked = apply_pattern(margin, margin_mask)
-    product, near_all = gather_product(masked, margin_masked, near_here)
+    run_ends = jnp.cumsum(atom_functions, dtype=jnp.int32)
+    bounds = jnp.stack([run_ends - atom_functions, run_ends])
+    product, near_all, pops = gather_product(masked, margin_masked, near_here, bounds)
     near = near_all[:, 0, :4]
-    strip_width = product.shape[1]
-    rows_global = row_index * rows_here + jnp.arange(rows_here, dtype=jnp.int32)
-    cols_global = (col_index * n_layer + layer_index) * strip_width + jnp.arange(
-        strip_width, dtype=jnp.int32
-    )
-    on_diagonal = rows_global[:, None] == cols_global[None, :]
-    diagonal_part = jnp.sum(jnp.where(on_diagonal, product, 0.0), axis=0)
-    run_ends = jnp.cumsum(atom_functions, dtype=jnp.int32)
-    run_starts = run_ends - atom_functions
-    member = (cols_global[:, None] >= run_starts[None, :]) & (
-        cols_global[:, None] < run_ends[None, :]
-    )
-    partial_pop = jnp.sum(jnp.where(member, diagonal_part[:, None], 0.0), axis=0)
-    all_pop = spread(partial_pop.reshape(-1, 128)).reshape(-1)
+    all_pop = pops.reshape(-1)
     index = jnp.arange(27, dtype=jnp.int32)
     near_atom = (
         ((row_index + index % 3 - 1) % n_row) * n_col + (col_index + index // 3 % 3 - 1) % n_col

time: 107 us -> 85.2 us (0.80)
  Pallas kernels: 95.3 us -> 74.8 us
    pallas_call x1 -> x0, Pallas kernels: 40.5 us -> none  [spread(): pl.pallas_call(spread_kernel, out_shape=jax.ShapeDtypeStruct(part.shape,...]
    pallas_call x1, Pallas kernels: 54.8 us -> 74.8 us  [gather_product(): pl.pallas_call(gather_kernel, out_shape=(jax.ShapeDtypeStruct((rows_here,...]
    reduce_sum x2 -> x0, other arithmetic: 1.44 us -> none  [the longest x1 0.75 us: shards(): jnp.sum(jnp.where(member, diagonal_part[:, None], 0.0), axis=0)]
    unnamed x12 -> x10, local copies, waits for them, and re-layouts: 2.76 us -> 2.08 us
where the time goes in v3:
time: 85.2 us; the launch traced here: 84.9 us
  Pallas kernels  74.8 us (88%)
  other arithmetic  4.51 us (5%)
  local copies, waits for them, and re-layouts  2.72 us (3%)
  between operations  1.45 us (2%)
  matrix products  1.43 us (2%)
    pallas_call x1, Pallas kernels, gather_product(): pl.pallas_call(gather_kernel, out_shape=(jax.ShapeDtypeStruct((rows_here,...  74.8 us
    unnamed x10, local copies, waits for them, and re-layouts  2.08 us

profile of v3, /device:TPU:1, one launch (start us, length us, event | category | flops | bytes accessed | tf_op | source)
XLA Modules:
  0.0 84.9 jit_solution(8037777515458575856)
XLA Ops:
  0.6 0.0 copy-start
  0.7 0.9 %dynamic-slice_convert_fusion = bf16[4,8]{1,0:T(4,128)(2,1)S(1)} fusion(s32[128,128]{1,0:T(8,128)} %param.9, s32[]{:T(128)S(6)} %select_n.139, s32[]{:T(128)S(6)} %select_n.141), kind=kLoop, calls=%fused_computation.40 | loop fusion | flops 32 | bytes 200 | tf_op jit(solution)/shard_map/convert_element_type | solution.py:503
  1.5 0.2 mul.159
  1.8 0.1 copy-done
  1.9 0.1 bitcast_multiply_fusion.margin_ref
  2.0 0.0 copy-start.1
  2.1 0.8 dynamic-slice_convert_fusion.1
  2.9 0.1 mul.153
  3.0 0.0 copy-start.2
  3.0 0.6 copy-done.2
  3.7 0.3 reduce-window.9
  4.0 0.1 slice.24
  4.1 0.1 slice_reduce_fusion
  4.2 0.1 bitcast_subtract_fusion
  5.0 0.0 copy-start.3
  5.0 0.6 copy-done.3
  5.6 0.6 fusion.25
  6.2 0.7 copy-done.4
  6.9 0.7 fusion.31
  7.6 74.8 %shard_map.86 = (f32[256,256]{1,0:T(8,128)S(1)}, f32[27,8,128]{2,1,0:T(8,128)S(1)}, f32[1,512]{1,0:T(1,128)S(1)}) custom-call(bf16[256,256]{1,0:T(8,128)(2,1)S(1)} %bitcast_multiply_fusion.1.density_ref, bf16[512,1024]{1,0:T(8,128)(2,1)S(1)} %bitcast_multiply_fusion.margin_ref, f32[8,128]{1,0:T(8,128)S(1)} %broadcast_in_dim.56.near_ref, ...), custom_call_target="tpu_custom_call" | custom-call | tf_op jit(solution)/shard_map/pallas_call | solution.py:404
  82.5 0.1 copy.11
  82.6 0.2 select_reduce_fusion
  82.8 1.4 %fusion = f32[32,32,128]{2,1,0:T(8,128)} fusion(f32[27,32]{0,1:T(8,128)S(1)} %get-tuple-element.15, f32[27,32]{0,1:T(8,128)S(1)} %get-tuple-element.14, f32[27]{0:T(128)S(1)} %get-tuple-element.12, f32[27]{0:T(128)S(1)} %get-tuple-element.10, s32[27]{0:T(128)S(1)} %add_multiply_fusion), kind=kOutput, calls=%fused_computation.1 | convolution fusion | flops 42522624 | bytes 531524 | tf_op jit(solution)/shard_map/axy,az->xyz/dot_general | solution.py:458
  84.3 0.7 convert_element_type.30
  (12 shorter events, 0.2 us)
Async XLA Ops:
  0.6 1.2 %copy-start = (bf16[512,1024]{1,0:T(8,128)(2,1)S(1)}, bf16[512,1024]{1,0:T(8,128)(2,1)}, u32[]{:S(2)}) copy-start(bf16[512,1024]{1,0:T(8,128)(2,1)} %param.8) | copy-start | bytes 3145732
  2.0 1.0 %copy-start.1 = (bf16[256,256]{1,0:T(8,128)(2,1)S(1)}, bf16[256,256]{1,0:T(8,128)(2,1)}, u32[]{:S(2)}) copy-start(bf16[256,256]{1,0:T(8,128)(2,1)} %param.7) | copy-start | bytes 393220
  3.0 0.7 copy-start.2
  5.0 0.7 copy-start.3
  6.2 0.7 copy-start.4

commit v4 on v3

--- a/solution.py
+++ b/solution.py
@@ -22,8 +22,9 @@
 
 
 def gather_kernel(
-    density_ref, margin_ref, near_ref, bounds_ref, product_ref, near_out, pops_out,
-    dens, marg, around, pops_home, pops_mine, pops_rows,
+    density_ref, margin_ref, functions_ref, kind_ref, offset_ref, exponents_ref,
+    product_ref, near_out, pops_out,
+    dens, marg, around, near_ref, bounds, pops_home, pops_mine, pops_rows,
     sem_spread, got_mine, sem_rows, got_rows, sem_around, got_around, sem_piece, sem_ring, sem_pair, got_slab, got_pair,
     sem_strip, sem_y, sem_half, got_strip, got_half,
 ):
@@ -83,6 +84,28 @@
         device = ((row + step) % n_row, col, layer)
         pl.semaphore_signal(barrier, inc=1, device_id=device, device_id_type=MESH)
 
+    lane = lax.broadcasted_iota(jnp.int32, near_ref.shape, 1)
+    values = jnp.where(lane == 0, exponents_ref[kind_ref[0]], 0.0)
+    for dim in range(3):
+        values = jnp.where(lane == dim + 1, offset_ref[dim, 0], values)
+    near_ref[...] = values
+
+    @pl.when(home)
+    def _():
+        atoms = functions_ref.shape[1]
+        functions = jnp.broadcast_to(functions_ref[...].astype(jnp.float32), (8, atoms))
+        square = (atoms, atoms)
+        before = lax.broadcasted_iota(jnp.int32, square, 0) < lax.broadcasted_iota(
+            jnp.int32, square, 1
+        )
+        starts = jnp.dot(
+            functions.astype(jnp.bfloat16),
+            jnp.where(before, 1.0, 0.0).astype(jnp.bfloat16),
+            preferred_element_type=jnp.float32,
+        )
+        bounds[0] = starts
+        bounds[1] = starts + functions
+
     @pl.when(home)
     def _():
         pl.semaphore_wait(barrier, 26 + 2 + 7 + n_row - 1 + members - 1)
@@ -188,53 +211,69 @@
         got = got_strip.at[kind * n_row + origin]
 
         def body():
-            copies = [
-                remote(block, block, sem_y.at[kind, other, way], got, (up, down)[way])
-                for way in range(2)
-            ]
             if start:
-                copies[0].wait_recv()
-            for copy in copies:
-                if start:
-                    copy.start()
+                remote(block, block, sem_y.at[kind, other, 0], got, up).wait_recv()
+            for way in range(2):
+                copy = remote(block, block, sem_y.at[kind, other, way], got, (up, down)[way])
+                send = copy.start if start else copy.wait_send
+                if kind == 1 and way == 1:
+                    when(y == 0, send)
                 else:
-                    copy.wait_send()
+                    send()
 
         when(live & (origin < rows_of[kind]), body)
 
     def next_strip(kind, other, way, start):
-        origin = 2 * ((y + (3 if way == 0 else 1)) % 4) + (x + other) % 2
+        origin_y = (y + (3 if way == 0 else 1)) % 4
+        origin = 2 * origin_y + (x + other) % 2
         whole = marg.at[kind * n_row + origin]
         block = marg.at[kind * n_row + origin, pl.ds(share // 2 * way, share // 2)]
 
         def body():
             if start:
                 remote(
-                    whole, whole, sem_y.at[kind, other, way], got_strip.at[kind * n_row + origin], up
+                    whole, whole, sem_y.at[kind, other, way],
+                    got_strip.at[kind * n_row + origin], up,
                 ).wait_recv()
-            copy = remote(
-                block, block, sem_half.at[kind, other, way],
-                got_half.at[kind * n_row + origin, way], (up, down)[way],
-            )
-            if start:
-                copy.start()
+            sent = sem_half.at[kind, other, way]
+            if kind == 0:
+                copy = remote(
+                    block, block, sent, got_half.at[origin, way], (up, down)[way]
+                )
+                (copy.start if start else copy.wait_send)()
             else:
-                copy.wait_send()
-
-        when(live & (origin < rows_of[kind]), body)
+                copy = remote(
+                    whole, whole, sent, got_strip.at[n_row + origin], (up, down)[way]
+                )
+                when(y == (2, 3)[way], copy.start if start else copy.wait_send)
+
+        if kind == 0:
+            when(live, body)
+        elif way == 0:
+            when(live & (origin_y < 2), body)
+        else:
+            when(live & (origin_y == 0), body)
 
     def far_strip(kind, xx):
         origin = 2 * ((y + 2) % 4) + xx
 
-        def body():
+        def halves():
             for way in range(2):
-                block = marg.at[kind * n_row + origin, pl.ds(share // 2 * way, share // 2)]
+                block = marg.at[origin, pl.ds(share // 2 * way, share // 2)]
                 remote(
-                    block, block, sem_half.at[kind, xx, way],
-                    got_half.at[kind * n_row + origin, way], up,
+                    block, block, sem_half.at[kind, xx, way], got_half.at[origin, way], up
                 ).wait_recv()
 
-        when(live & (origin < rows_of[kind]), body)
+        def whole():
+            block = marg.at[n_row + origin]
+            remote(
+                block, block, sem_half.at[kind, xx, 0], got_strip.at[n_row + origin], up
+            ).wait_recv()
+
+        if kind == 0:
+            when(live, halves)
+        else:
+            when(live & (y >= 2), whole)
 
     def nexts(kind, other, start):
         for way in range(2):
@@ -332,7 +371,8 @@
                 )
             return carry
 
-        lax.fori_loop(0, marg.shape[0], add_share, 0)
+        shares = marg.shape[0] - jnp.where(y == 0, 2, 0)
+        lax.fori_loop(0, shares, add_share, 0)
 
     @pl.when(jnp.logical_not(live))
     def _():
@@ -343,9 +383,10 @@
         side = product_ref.shape
         here = lax.broadcasted_iota(jnp.int32, side, 0) == lax.broadcasted_iota(jnp.int32, side, 1)
         diagonal = jnp.sum(jnp.where(here, product_ref[...], 0.0), axis=1, keepdims=True)
-        wide = (side[0], bounds_ref.shape[1])
+        wide = (side[0], functions_ref.shape[1])
         function = lax.broadcasted_iota(jnp.int32, wide, 0) + row * side[0]
-        member = (function >= bounds_ref[0:1, :]) & (function < bounds_ref[1:2, :])
+        function = function.astype(jnp.float32)
+        member = (function >= bounds[0, 0:1, :]) & (function < bounds[1, 0:1, :])
         pops_home[...] = jnp.sum(jnp.where(member, diagonal, 0.0), axis=0, keepdims=True)
 
     for index in range(27):
@@ -391,32 +432,36 @@
         copy.wait_send()
 
 
-def gather_product(density, margin, near, bounds):
+def gather_product(density, margin, functions, kind, offset, exponents):
     rows_here, piece_width = density.shape
     share, share_cols = margin.shape
     n_row, n_col, n_layer = (lax.axis_size(axis) for axis in ("row", "col", "layer"))
     depth = n_row * rows_here + REACH * BLK
     strip = share_cols // n_layer
     dma = pltpu.SemaphoreType.DMA
+    near, atoms = (1, 128), functions.shape[0]
     vmem = pl.BlockSpec(memory_space=pltpu.VMEM)
+    smem = pl.BlockSpec(memory_space=pltpu.SMEM)
     anywhere = pl.BlockSpec(memory_space=pl.ANY)
     pieces, shares = depth // piece_width, depth // share
     return pl.pallas_call(
         gather_kernel,
         out_shape=(
             jax.ShapeDtypeStruct((rows_here, strip), jnp.float32),
-            jax.ShapeDtypeStruct((27,) + near.shape, jnp.float32),
-            jax.ShapeDtypeStruct((1, bounds.shape[1]), jnp.float32),
+            jax.ShapeDtypeStruct((27,) + near, jnp.float32),
+            jax.ShapeDtypeStruct((1, atoms), jnp.float32),
         ),
-        in_specs=[anywhere, anywhere, vmem, vmem],
+        in_specs=[anywhere, anywhere, vmem, smem, smem, smem],
         out_specs=(vmem, vmem, vmem),
         scratch_shapes=[
             pltpu.VMEM((pieces, rows_here, piece_width), jnp.bfloat16),
             pltpu.VMEM((shares, share, strip), jnp.bfloat16),
-            pltpu.VMEM((27,) + near.shape, jnp.float32),
-            pltpu.VMEM((1, bounds.shape[1]), jnp.float32),
-            pltpu.VMEM((1, bounds.shape[1]), jnp.float32),
-            pltpu.VMEM((n_row, 1, bounds.shape[1]), jnp.float32),
+            pltpu.VMEM((27,) + near, jnp.float32),
+            pltpu.VMEM(near, jnp.float32),
+            pltpu.VMEM((2, 8, atoms), jnp.float32),
+            pltpu.VMEM((1, atoms), jnp.float32),
+            pltpu.VMEM((1, atoms), jnp.float32),
+            pltpu.VMEM((n_row, 1, atoms), jnp.float32),
             dma((n_col * n_layer,)),
             dma,
             dma((n_row,)),
@@ -432,12 +477,12 @@
             dma((2, 2, 2)),
             dma((2, 2, 2)),
             dma((shares,)),
-            dma((shares, 2)),
+            dma((n_row, 2)),
         ],
         compiler_params=pltpu.CompilerParams(
             collective_id=1, has_side_effects=True, vmem_limit_bytes=24 * 1024 * 1024
         ),
-    )(density, margin, near, bounds)
+    )(density, margin, functions.reshape(1, -1), kind, offset, exponents)
 
 
 def near_profile(cells, tile_of, extent, offset, exponent_of):
@@ -467,9 +512,6 @@
     row_index = lax.axis_index("row")
     col_index = lax.axis_index("col")
     layer_index = lax.axis_index("layer")
-    exponent_here = kind_exponent(atom_kind, exponents)
-    near_here = jnp.concatenate([exponent_here[:, None], atom_offset.T], axis=1)
-    near_here = jnp.broadcast_to(jnp.pad(near_here, ((0, 0), (0, 124))), (8, 128))
     density_mask = lax.dynamic_slice(
         block_pattern,
         (row_index * (rows_here // BLK), (layer_index * n_col + col_index) * piece_width // BLK),
@@ -482,9 +524,9 @@
         (share_rows // BLK, share_cols // BLK),
     )
     margin_masked = apply_pattern(margin, margin_mask)
-    run_ends = jnp.cumsum(atom_functions, dtype=jnp.int32)
-    bounds = jnp.stack([run_ends - atom_functions, run_ends])
-    product, near_all, pops = gather_product(masked, margin_masked, near_here, bounds)
+    product, near_all, pops = gather_product(
+        masked, margin_masked, atom_functions, atom_kind, atom_offset, exponents
+    )
     near = near_all[:, 0, :4]
     all_pop = pops.reshape(-1)
     index = jnp.arange(27, dtype=jnp.int32)
@@ -504,6 +546,49 @@
     return (shaped * gate_mask[:, None, :, None]).reshape(matrix.shape)
 
 
+def shards(density, margin, block_pattern, atom_functions, atom_kind, atom_offset, exponents):
+    rows_here, piece_width = density.shape
+    share_rows, share_cols = margin.shape
+    n_row = lax.axis_size("row")
+    n_col = lax.axis_size("col")
+    n_layer = lax.axis_size("layer")
+    row_index = lax.axis_index("row")
+    col_index = lax.axis_index("col")
+    layer_index = lax.axis_index("layer")
+    density_mask = lax.dynamic_slice(
+        block_pattern,
+        (row_index * (rows_here // BLK), (layer_index * n_col + col_index) * piece_width // BLK),
+        (rows_here // BLK, piece_width // BLK),
+    )
+    masked = apply_pattern(density, density_mask)
+    margin_mask = lax.dynamic_slice(
+        block_pattern,
+        ((layer_index * n_row + row_index) * share_rows // BLK, col_index * share_cols // BLK),
+        (share_rows // BLK, share_cols // BLK),
+    )
+    margin_masked = apply_pattern(margin, margin_mask)
+    product, near_all, pops = gather_product(
+        masked, margin_masked, atom_functions, atom_kind, atom_offset, exponents
+    )
+    near = near_all[:, 0, :4]
+    all_pop = pops.reshape(-1)
+    index = jnp.arange(27, dtype=jnp.int32)
+    near_atom = (
+        ((row_index + index % 3 - 1) % n_row) * n_col + (col_index + index // 3 % 3 - 1) % n_col
+    ) * n_layer + (layer_index + index // 9 - 1) % n_layer
+    atoms = jnp.arange(all_pop.shape[0], dtype=jnp.int32)
+    weights = jnp.sum(jnp.where(near_atom[:, None] == atoms[None, :], all_pop[None, :], 0.0), axis=1)
+    return (product.astype(jnp.bfloat16), collocate(near, weights))
+
+
+def apply_pattern(matrix, pattern_part):
+    row_blocks = matrix.shape[0] // BLK
+    col_blocks = matrix.shape[1] // BLK
+    shaped = matrix.reshape(row_blocks, BLK, col_blocks, BLK)
+    gate_mask = pattern_part.astype(jnp.bfloat16)
+    return (shaped * gate_mask[:, None, :, None]).reshape(matrix.shape)
+
+
 def kind_exponent(kinds_of, exponents):
     kind_match = kinds_of[:, None] == jnp.arange(exponents.shape[0], dtype=jnp.int32)[None, :]
     return jnp.sum(jnp.where(kind_match, exponents[None, :], 0.0), axis=1)

time: 85.2 us -> 84.1 us (0.987)
  other arithmetic: 4.51 us -> 2.77 us
  Pallas kernels: 74.8 us -> 76.3 us
    pallas_call x1, Pallas kernels: 74.8 us -> 76.3 us  [gather_product(): pl.pallas_call(gather_kernel, out_shape=(jax.ShapeDtypeStruct((rows_here,...]
    unnamed x10 -> x11, local copies, waits for them, and re-layouts: 2.08 us -> 1.49 us
where the time goes in v4:
time: 84.1 us; the launch traced here: 83.8 us
  Pallas kernels  76.3 us (91%)
  other arithmetic  2.77 us (3%)
  local copies, waits for them, and re-layouts  1.92 us (2%)
  between operations  1.46 us (2%)
  matrix products  1.44 us (2%)
    pallas_call x1, Pallas kernels, gather_product(): pl.pallas_call(gather_kernel, out_shape=(jax.ShapeDtypeStruct((rows_here,...  76.3 us

profile of v4, /device:TPU:1, one launch (start us, length us, event | category | flops | bytes accessed | tf_op | source)
XLA Modules:
  0.0 83.8 jit_solution(11516131913326027122)
XLA Ops:
  0.6 0.0 copy-start.2
  0.7 0.9 %dynamic-slice_convert_fusion = bf16[4,8]{1,0:T(4,128)(2,1)S(1)} fusion(s32[128,128]{1,0:T(8,128)} %param.9, s32[]{:T(128)S(6)} %select_n.134, s32[]{:T(128)S(6)} %select_n.136), kind=kLoop, calls=%fused_computation.37 | loop fusion | flops 32 | bytes 200 | tf_op jit(solution)/shard_map/convert_element_type | solution.py:588
  1.5 0.2 mul.159
  1.8 0.1 copy-done.2
  1.9 0.1 bitcast_multiply_fusion.margin_ref
  2.0 0.0 copy-start.3
  2.1 0.8 dynamic-slice_convert_fusion.1
  2.9 0.1 mul.153
  3.0 0.0 copy-done.3
  3.0 0.0 copy-start.4
  3.0 0.6 copy-done.4
  3.7 0.1 copy.11.offset_ref
  3.8 0.0 copy-start
  4.4 0.0 copy-start.1
  4.4 0.0 copy-done
  4.4 0.6 copy-done.1
  5.1 76.3 %shard_map.86 = (f32[256,256]{1,0:T(8,128)S(1)}, f32[27,1,128]{2,1,0:T(1,128)S(1)}, f32[1,512]{1,0:T(1,128)S(1)}) custom-call(bf16[256,256]{1,0:T(8,128)(2,1)S(1)} %bitcast_multiply_fusion.1.density_ref, bf16[512,1024]{1,0:T(8,128)(2,1)S(1)} %bitcast_multiply_fusion.margin_ref, s32[1,512]{1,0:T(1,128)S(1)} %bitcast.24, s32[1]{0:T(128)S(6)} %copy.17.kind_ref, ...), custom_call_target="tpu_custom_call" | custom-call | tf_op jit(solution)/shard_map/pallas_call | solution.py:447
  81.4 0.2 select_reduce_fusion
  81.6 0.1 copy.12
  81.7 1.4 %fusion = f32[32,32,128]{2,1,0:T(8,128)} fusion(f32[27,32]{0,1:T(8,128)S(1)} %get-tuple-element.13, f32[27,32]{0,1:T(8,128)S(1)} %get-tuple-element.12, f32[27]{0:T(128)S(1)} %get-tuple-element.10, f32[27]{0:T(128)S(1)} %get-tuple-element.8, s32[27]{0:T(128)S(1)} %add_multiply_fusion), kind=kOutput, calls=%fused_computation.1 | convolution fusion | flops 42522624 | bytes 531524 | tf_op jit(solution)/shard_map/axy,az->xyz/dot_general | solution.py:503
  83.2 0.7 convert_element_type.28
  (6 shorter events, 0.1 us)
Async XLA Ops:
  0.6 1.2 %copy-start.2 = (bf16[512,1024]{1,0:T(8,128)(2,1)S(1)}, bf16[512,1024]{1,0:T(8,128)(2,1)}, u32[]{:S(2)}) copy-start(bf16[512,1024]{1,0:T(8,128)(2,1)} %param.8) | copy-start | bytes 3145732
  2.0 1.0 %copy-start.3 = (bf16[256,256]{1,0:T(8,128)(2,1)S(1)}, bf16[256,256]{1,0:T(8,128)(2,1)}, u32[]{:S(2)}) copy-start(bf16[256,256]{1,0:T(8,128)(2,1)} %param.7) | copy-start | bytes 393220
  3.0 0.7 copy-start.4
  3.8 0.7 copy-start
  4.4 0.7 copy-start.1

commit v5 on v4

--- a/solution.py
+++ b/solution.py
@@ -24,7 +24,7 @@
 def gather_kernel(
     density_ref, margin_ref, functions_ref, kind_ref, offset_ref, exponents_ref,
     product_ref, near_out, pops_out,
-    dens, marg, around, near_ref, bounds, pops_home, pops_mine, pops_rows,
+    dens, marg, hops, sem_hop, got_hop, sem_onto, around, near_ref, bounds, pops_home, pops_mine, pops_rows,
     sem_spread, got_mine, sem_rows, got_rows, sem_around, got_around, sem_piece, sem_ring, sem_pair, got_slab, got_pair,
     sem_strip, sem_y, sem_half, got_strip, got_half,
 ):
@@ -54,7 +54,7 @@
     shifts = [
         (dr, dc, dl) for dl in (-1, 0, 1) for dc in (-1, 0, 1) for dr in (-1, 0, 1)
     ]
-    plane = [(0, 2), (1, 2), (0, 3), (1, 3), (0, 0), (0, 1), (1, 0), (1, 1)]
+    plane = [(0, 2), (1, 2), (0, 3), (1, 3), (0, 0), (0, 1)]
     home_col, home_layer = row // n_layer, row % n_layer
     home = (col == home_col) & (layer == home_layer)
     members = n_col * n_layer
@@ -138,6 +138,36 @@
             when(here, pltpu.make_async_copy(source, slot, got).start)
         when(jnp.logical_not(here), far.start if start else far.wait_send)
 
+    def hop_copy(kind, ll, side, start):
+        slot = 2 * kind + x
+        far = remote(
+            margin_ref.at[pl.ds(share // 2 * side, share // 2), pl.ds(strip * ll, strip)],
+            hops.at[slot], sem_hop.at[ll, side], got_hop.at[slot],
+            (2 * y + (x + side) % 2, col, 2 + ll),
+        )
+        (far.start if start else far.wait_send)()
+
+    def hop_onto(kind, side, start):
+        origin = (x + side) % 2
+        slot = 2 * kind + origin
+        block = hops.at[slot]
+
+        def body():
+            target = marg.at[
+                kind * n_row + 2 * y + origin, pl.ds(share // 2 * side, share // 2)
+            ]
+            copy = remote(
+                block, target, sem_onto.at[slot], got_strip.at[kind * n_row + 2 * y + origin],
+                (2 * y + 1 - origin, col, layer - 2),
+            )
+            if start:
+                remote(block, block, sem_onto.at[slot], got_hop.at[slot], up).wait_recv()
+                copy.start()
+            else:
+                copy.wait_send()
+
+        when(live & (2 * y + origin < rows_of[kind]), body)
+
     def first_copies(start):
         for kind in range(2):
 
@@ -146,6 +176,9 @@
                     piece_copy(kind, ll, start)
 
             def strips(kind=kind):
+                for ll in range(2):
+                    for side in range(2):
+                        hop_copy(kind, ll, side, start)
                 for target in plane:
                     strip_copy(kind, target, start)
 
@@ -287,20 +320,24 @@
         ring_step(2, start)
         nexts(0, 0, start)
         ring_step(3, start)
+        own_strip(0, 1, start)
         ring_step(4, start)
         nexts(1, 0, start)
+        own_strip(1, 1, start)
         ring_step(5, start)
         ring_step(6, start)
-        own_strip(0, 1, start)
         ring_step(7, start)
         ring_step(8, start)
-        own_strip(1, 1, start)
         nexts(0, 1, start)
         nexts(1, 1, start)
 
     def relays_high(start):
         ring_step(0, start)
+        hop_onto(0, 0, start)
+        hop_onto(0, 1, start)
         ring_step(1, start)
+        hop_onto(1, 0, start)
+        hop_onto(1, 1, start)
         own_strip(0, 1, start)
         ring_step(2, start)
         own_strip(0, 0, start)
@@ -456,6 +493,10 @@
         scratch_shapes=[
             pltpu.VMEM((pieces, rows_here, piece_width), jnp.bfloat16),
             pltpu.VMEM((shares, share, strip), jnp.bfloat16),
+            pltpu.VMEM((4, share // 2, strip), jnp.bfloat16),
+            dma((2, 2)),
+            dma((4,)),
+            dma((4,)),
             pltpu.VMEM((27,) + near, jnp.float32),
             pltpu.VMEM(near, jnp.float32),
             pltpu.VMEM((2, 8, atoms), jnp.float32),

time: 84.1 us -> 84.2 us (level)
  no operation moved by 1% of the time
where the time goes in v5:
time: 84.2 us; the launch traced here: 83.9 us
  Pallas kernels  76.4 us (91%)
  other arithmetic  2.77 us (3%)
  local copies, waits for them, and re-layouts  1.92 us (2%)
  between operations  1.46 us (2%)
  matrix products  1.44 us (2%)
    pallas_call x1, Pallas kernels, gather_product(): pl.pallas_call(gather_kernel, out_shape=(jax.ShapeDtypeStruct((rows_here,...  76.4 us

profile of v5, /device:TPU:1, one launch (start us, length us, event | category | flops | bytes accessed | tf_op | source)
XLA Modules:
  0.0 83.9 jit_solution(11003883323614538931)
XLA Ops:
  0.6 0.0 copy-start.2
  0.7 0.9 %dynamic-slice_convert_fusion = bf16[4,8]{1,0:T(4,128)(2,1)S(1)} fusion(s32[128,128]{1,0:T(8,128)} %param.9, s32[]{:T(128)S(6)} %select_n.134, s32[]{:T(128)S(6)} %select_n.136), kind=kLoop, calls=%fused_computation.37 | loop fusion | flops 32 | bytes 200 | tf_op jit(solution)/shard_map/convert_element_type | solution.py:629
  1.5 0.2 mul.159
  1.8 0.1 copy-done.2
  1.9 0.1 bitcast_multiply_fusion.margin_ref
  2.0 0.0 copy-start.3
  2.1 0.8 dynamic-slice_convert_fusion.1
  2.9 0.1 mul.153
  3.0 0.0 copy-done.3
  3.0 0.0 copy-start.4
  3.0 0.6 copy-done.4
  3.7 0.1 copy.11.offset_ref
  3.8 0.0 copy-start
  4.4 0.0 copy-start.1
  4.4 0.0 copy-done
  4.4 0.6 copy-done.1
  5.1 76.4 %shard_map.86 = (f32[256,256]{1,0:T(8,128)S(1)}, f32[27,1,128]{2,1,0:T(1,128)S(1)}, f32[1,512]{1,0:T(1,128)S(1)}) custom-call(bf16[256,256]{1,0:T(8,128)(2,1)S(1)} %bitcast_multiply_fusion.1.density_ref, bf16[512,1024]{1,0:T(8,128)(2,1)S(1)} %bitcast_multiply_fusion.margin_ref, s32[1,512]{1,0:T(1,128)S(1)} %bitcast.24, s32[1]{0:T(128)S(6)} %copy.17.kind_ref, ...), custom_call_target="tpu_custom_call" | custom-call | tf_op jit(solution)/shard_map/pallas_call | solution.py:484
  81.5 0.2 select_reduce_fusion
  81.7 0.1 copy.12
  81.8 1.4 %fusion = f32[32,32,128]{2,1,0:T(8,128)} fusion(f32[27,32]{0,1:T(8,128)S(1)} %get-tuple-element.13, f32[27,32]{0,1:T(8,128)S(1)} %get-tuple-element.12, f32[27]{0:T(128)S(1)} %get-tuple-element.10, f32[27]{0:T(128)S(1)} %get-tuple-element.8, s32[27]{0:T(128)S(1)} %add_multiply_fusion), kind=kOutput, calls=%fused_computation.1 | convolution fusion | flops 42522624 | bytes 531524 | tf_op jit(solution)/shard_map/axy,az->xyz/dot_general | solution.py:544
  83.3 0.7 convert_element_type.28
  (6 shorter events, 0.1 us)
Async XLA Ops:
  0.6 1.2 %copy-start.2 = (bf16[512,1024]{1,0:T(8,128)(2,1)S(1)}, bf16[512,1024]{1,0:T(8,128)(2,1)}, u32[]{:S(2)}) copy-start(bf16[512,1024]{1,0:T(8,128)(2,1)} %param.8) | copy-start | bytes 3145732
  2.0 1.0 %copy-start.3 = (bf16[256,256]{1,0:T(8,128)(2,1)S(1)}, bf16[256,256]{1,0:T(8,128)(2,1)}, u32[]{:S(2)}) copy-start(bf16[256,256]{1,0:T(8,128)(2,1)} %param.7) | copy-start | bytes 393220
  3.0 0.7 copy-start.4
  3.8 0.7 copy-start
  4.4 0.7 copy-start.1

commit v6 on v4

--- a/solution.py
+++ b/solution.py
@@ -355,28 +355,34 @@
     for kind in range(2):
         for origin in range(cols_of[kind]):
             pair_wait(kind, origin)
+    product_ref[...] = jnp.zeros_like(product_ref)
+
+    def add_shares(offset):
+        origin_y = (y + offset) % 4
+
+        def add(kind):
+            def add_share(xx, carry):
+                j = kind * n_row + 2 * origin_y + xx
+                for side in range(2):
+                    product_ref[...] += jnp.dot(
+                        dens[2 * j + side],
+                        marg[j, pl.ds(share // 2 * side, share // 2)],
+                        preferred_element_type=jnp.float32,
+                    )
+                return carry
+
+            lax.fori_loop(0, 2, add_share, 0)
+
+        when(live, lambda: add(0))
+        coupled = (origin_y == 0) | ((origin_y == 1) & (y > 0))
+        when(live & coupled, lambda: add(1))
+
+    for offset in (0, 1, 3):
+        add_shares(offset)
+    for kind in range(2):
         for xx in range(2):
             far_strip(kind, xx)
-
-    @pl.when(live)
-    def _():
-        product_ref[...] = jnp.zeros_like(product_ref)
-
-        def add_share(j, carry):
-            for side in range(2):
-                product_ref[...] += jnp.dot(
-                    dens[2 * j + side],
-                    marg[j, pl.ds(share // 2 * side, share // 2)],
-                    preferred_element_type=jnp.float32,
-                )
-            return carry
-
-        shares = marg.shape[0] - jnp.where(y == 0, 2, 0)
-        lax.fori_loop(0, shares, add_share, 0)
-
-    @pl.when(jnp.logical_not(live))
-    def _():
-        product_ref[...] = jnp.zeros_like(product_ref)
+    add_shares(2)
 
     @pl.when(home)
     def _():

time: 84.1 us -> 82.2 us (0.977)
  Pallas kernels: 76.3 us -> 74.4 us
    pallas_call x1, Pallas kernels: 76.3 us -> 74.4 us  [gather_product(): pl.pallas_call(gather_kernel, out_shape=(jax.ShapeDtypeStruct((rows_here,...]
where the time goes in v6:
time: 82.2 us; the launch traced here: 82 us
  Pallas kernels  74.4 us (91%)
  other arithmetic  2.77 us (3%)
  local copies, waits for them, and re-layouts  1.92 us (2%)
  between operations  1.46 us (2%)
  matrix products  1.43 us (2%)
    pallas_call x1, Pallas kernels, gather_product(): pl.pallas_call(gather_kernel, out_shape=(jax.ShapeDtypeStruct((rows_here,...  74.4 us
    convert_element_type x2, other arithmetic, apply_pattern(): gate_mask = pattern_part.astype(jnp.bfloat16)  1.66 us

profile of v6, /device:TPU:1, one launch (start us, length us, event | category | flops | bytes accessed | tf_op | source)
XLA Modules:
  0.0 82.0 jit_solution(12261553020467750391)
XLA Ops:
  0.6 0.0 copy-start.2
  0.7 0.9 %dynamic-slice_convert_fusion = bf16[4,8]{1,0:T(4,128)(2,1)S(1)} fusion(s32[128,128]{1,0:T(8,128)} %param.9, s32[]{:T(128)S(6)} %select_n.134, s32[]{:T(128)S(6)} %select_n.136), kind=kLoop, calls=%fused_computation.37 | loop fusion | flops 32 | bytes 200 | tf_op jit(solution)/shard_map/convert_element_type | solution.py:594
  1.5 0.2 mul.159
  1.8 0.1 copy-done.2
  1.9 0.1 bitcast_multiply_fusion.margin_ref
  2.0 0.0 copy-start.3
  2.1 0.8 dynamic-slice_convert_fusion.1
  2.9 0.1 mul.153
  3.0 0.0 copy-done.3
  3.0 0.0 copy-start.4
  3.0 0.6 copy-done.4
  3.7 0.1 copy.11.offset_ref
  3.8 0.0 copy-start
  4.4 0.0 copy-start.1
  4.4 0.0 copy-done
  4.4 0.6 copy-done.1
  5.1 74.4 %shard_map.86 = (f32[256,256]{1,0:T(8,128)S(1)}, f32[27,1,128]{2,1,0:T(1,128)S(1)}, f32[1,512]{1,0:T(1,128)S(1)}) custom-call(bf16[256,256]{1,0:T(8,128)(2,1)S(1)} %bitcast_multiply_fusion.1.density_ref, bf16[512,1024]{1,0:T(8,128)(2,1)S(1)} %bitcast_multiply_fusion.margin_ref, s32[1,512]{1,0:T(1,128)S(1)} %bitcast.24, s32[1]{0:T(128)S(6)} %copy.17.kind_ref, ...), custom_call_target="tpu_custom_call" | custom-call | tf_op jit(solution)/shard_map/pallas_call | solution.py:453
  79.6 0.2 select_reduce_fusion
  79.7 0.1 copy.12
  79.9 1.4 %fusion = f32[32,32,128]{2,1,0:T(8,128)} fusion(f32[27,32]{0,1:T(8,128)S(1)} %get-tuple-element.13, f32[27,32]{0,1:T(8,128)S(1)} %get-tuple-element.12, f32[27]{0:T(128)S(1)} %get-tuple-element.10, f32[27]{0:T(128)S(1)} %get-tuple-element.8, s32[27]{0:T(128)S(1)} %add_multiply_fusion), kind=kOutput, calls=%fused_computation.1 | convolution fusion | flops 42522624 | bytes 531524 | tf_op jit(solution)/shard_map/axy,az->xyz/dot_general | solution.py:509
  81.3 0.7 convert_element_type.28
  (6 shorter events, 0.1 us)
Async XLA Ops:
  0.6 1.2 %copy-start.2 = (bf16[512,1024]{1,0:T(8,128)(2,1)S(1)}, bf16[512,1024]{1,0:T(8,128)(2,1)}, u32[]{:S(2)}) copy-start(bf16[512,1024]{1,0:T(8,128)(2,1)} %param.8) | copy-start | bytes 3145732
  2.0 1.0 %copy-start.3 = (bf16[256,256]{1,0:T(8,128)(2,1)S(1)}, bf16[256,256]{1,0:T(8,128)(2,1)}, u32[]{:S(2)}) copy-start(bf16[256,256]{1,0:T(8,128)(2,1)} %param.7) | copy-start | bytes 393220
  3.0 0.7 copy-start.4
  3.8 0.7 copy-start
  4.4 0.7 copy-start.1
